TPU v7x, 512 devices: a whole 4x8x8 slice. The times are simulated.
512 devices in a mesh: gx: 16 (over x_lo, z), gy: 4 (over x_hi, core), gz: 8 (over y).
Axes of the slice: x: 4 (x_hi: 2, x_lo: 2; x = x_hi * 2 + x_lo), y: 8, z: 8, core: 2. Of those that a mesh axis runs over, the one named last changes fastest.
Arguments:
- gas: float32 [6, 128, 32, 1024], P(None, 'gx', 'gy', 'gz'), may hold values from -1.5 to 6, as said below
- parcels: float32 [32768, 5, 128], P(('gx', 'gy', 'gz')), may hold values from -1 to 2, as said below
- home_cell_index: int32 [32768, 128], P(('gx', 'gy', 'gz')), may hold values from 0 to 8191
- order: int32 [512, 64], P(('gx', 'gy', 'gz')), may hold values from 0 to 63, each once within a row
- counts: int32 [512, 3], P(('gx', 'gy', 'gz')), may hold values from 0 to 32, as said below
Outputs:
- gas_out: float32 [6, 128, 32, 1024], P(None, 'gx', 'gy', 'gz')
- moved_parcels: float32 [32768, 5, 128], P(('gx', 'gy', 'gz'))
Inputs may be any that keep to these rules, and one draw needn't show every extreme that they name: `gas`: gas density lies in 0.8 to 1.6, pressure in 0.8 to 1.6, velocities within 0.8, vapour fraction in 0.05 to 0.3. `parcels`: parcel masses lie in 0.2 to 2, temperatures in 0.3 to 1.2, velocities in -1 to 1.5. `counts`: kept is at most 32, forward and back each at most 16; each bound is reached in every draw.
All inputs are finite; a program needn't handle non-finite values.
Results may differ from a plain program's by a relative error of at most 0.00002.
Values sent between devices are 32-bit elements; how exact they have to be, the bound alone decides.
No kernel may reach another device: no remote copies, remote signals or barrier semaphores. Data moves between devices by JAX's collectives and lax.ppermute only.
A program may use at most 64 MiB of HBM per device.

v0:
```python
import jax
import jax.numpy as jnp
from jax import lax
from jax.sharding import PartitionSpec as P

GAMMA = 1.4
TIME_STEP = 0.1
RATE = 3.0
ACTIVATION = 2.0
HEAT = 5.0
DRAG_RELAX_TIME = 0.4
HEATING_RELAX = 0.6
EVAP_RATE = 1.5
LIQUID_HEAT = 2.0


def padded_2(cells, sides, width):
    for axis, dim in sides:
        count = lax.axis_size(axis)
        ends = count - 1
        head = lax.slice_in_dim(cells, 0, width, axis=dim)
        tail = lax.slice_in_dim(cells, cells.shape[dim] - width, cells.shape[dim], axis=dim)
        cells = jnp.concatenate(
            [
                lax.ppermute(tail, axis, [(i, (i + 1) % count) for i in range(ends)]),
                cells,
                lax.ppermute(head, axis, [((i + 1) % count, i) for i in range(ends)]),
            ],
            axis=dim,
        )
    return cells


def from_behind(block, axis, distance):
    devices = range(lax.axis_size(axis))
    route = [(i - distance, i) for i in devices if i - distance in devices]
    return lax.ppermute(block, axis, route)


def pressure_of(gas_state):
    motion_energy = (
        gas_state[1] * gas_state[1] + gas_state[2] * gas_state[2] + gas_state[3] * gas_state[3]
    )
    return (GAMMA - 1.0) * (gas_state[4] - 0.5 * motion_energy / gas_state[0])


def directional(column, direction):
    density = column[0]
    speed_along = column[1 + direction] / density
    pressure = pressure_of(column)
    pieces = [
        column[1 + direction],
        column[1] * speed_along,
        column[2] * speed_along,
        column[3] * speed_along,
        (column[4] + pressure) * speed_along,
        column[5] * speed_along,
    ]
    pieces[1 + direction] = pieces[1 + direction] + pressure
    return (jnp.stack(pieces), jnp.abs(speed_along) + jnp.sqrt(GAMMA * pressure / density))


def tendency(padded):
    interior = padded[:, 1:-1, 1:-1, 1:-1]
    result = jnp.zeros_like(interior)
    for direction in range(3):
        window = [slice(None), slice(1, -1), slice(1, -1), slice(1, -1)]
        window[direction + 1] = slice(None)
        column = padded[tuple(window)]
        fluxes, speeds = directional(column, direction)
        array_dim = direction + 1
        length = column.shape[array_dim]
        lower_flux = lax.slice_in_dim(fluxes, 0, length - 1, axis=array_dim)
        upper_flux = lax.slice_in_dim(fluxes, 1, length, axis=array_dim)
        lower_speed = lax.slice_in_dim(speeds, 0, length - 1, axis=direction)
        upper_speed = lax.slice_in_dim(speeds, 1, length, axis=direction)
        left_neighbor_fields = lax.slice_in_dim(column, 0, length - 1, axis=array_dim)
        upper_state = lax.slice_in_dim(column, 1, length, axis=array_dim)
        face_flux = 0.5 * (lower_flux + upper_flux) - 0.5 * jnp.maximum(lower_speed, upper_speed)[
            None
        ] * (upper_state - left_neighbor_fields)
        result = result - (
            lax.slice_in_dim(face_flux, 1, length - 1, axis=array_dim)
            - lax.slice_in_dim(face_flux, 0, length - 2, axis=array_dim)
        )
    burned = RATE * interior[5] * jnp.exp(-ACTIVATION * interior[0] / pressure_of(interior))
    result = result.at[4].add(HEAT * burned)
    result = result.at[5].add(-burned)
    return result


def parcel_update(parcels, transported):
    density = transported[0]
    gas_velocity = transported[1:4] / density
    gas_temp = pressure_of(transported) / density
    vapour = transported[5] / density
    drop_velocity = jnp.moveaxis(parcels[:, 0:3], 1, 0)
    drop_mass = parcels[:, 3]
    drop_temp = parcels[:, 4]
    root_mass = jnp.sqrt(drop_mass)
    new_mass = drop_mass * jnp.exp(
        -TIME_STEP * EVAP_RATE * gas_temp / (root_mass * (1.0 + vapour * vapour))
    )
    new_velocity = gas_velocity + (drop_velocity - gas_velocity) * jnp.exp(
        -TIME_STEP / (DRAG_RELAX_TIME * root_mass)
    )
    new_temp = gas_temp + (drop_temp - gas_temp) * jnp.exp(-TIME_STEP / (HEATING_RELAX * root_mass))
    mass_source = drop_mass - new_mass
    momentum_source = drop_mass * drop_velocity - new_mass * new_velocity
    energy_source = 0.5 * (
        drop_mass * jnp.sum(drop_velocity * drop_velocity, axis=0)
        - new_mass * jnp.sum(new_velocity * new_velocity, axis=0)
    ) + LIQUID_HEAT * (drop_mass * drop_temp - new_mass * new_temp)
    sources = jnp.stack(
        [
            mass_source,
            momentum_source[0],
            momentum_source[1],
            momentum_source[2],
            energy_source,
            mass_source,
        ]
    )
    updated = jnp.stack(
        [new_velocity[0], new_velocity[1], new_velocity[2], new_mass, new_temp], axis=1
    )
    return (updated, sources)


def clamp_edges(padded, width, edges):
    for direction in range(3):
        array_dim = direction + 1
        length = padded.shape[array_dim]
        at_first, at_last = edges[direction]
        low_cell = lax.slice_in_dim(padded, width, width + 1, axis=array_dim)
        high_cell = lax.slice_in_dim(padded, length - width - 1, length - width, axis=array_dim)
        marker_shape = [1, 1, 1, 1]
        marker_shape[array_dim] = length
        occupancy_flag = lax.broadcasted_iota(jnp.int32, tuple(marker_shape), array_dim)
        padded = jnp.where(at_first & (occupancy_flag < width), low_cell, padded)
        padded = jnp.where(at_last & (occupancy_flag >= length - width), high_cell, padded)
    return padded


def padded_one(gas_state, edges):
    padded = padded_2(gas_state, (("gx", 1), ("gy", 2), ("gz", 3)), 1)
    return clamp_edges(padded, 1, edges)


def body(gas, parcels, home_cell_index, order, counts):
    edges = (
        (lax.axis_index("gx") == 0, lax.axis_index("gx") == lax.axis_size("gx") - 1),
        (lax.axis_index("gy") == 0, lax.axis_index("gy") == lax.axis_size("gy") - 1),
        (lax.axis_index("gz") == 0, lax.axis_index("gz") == lax.axis_size("gz") - 1),
    )
    section_one = gas + TIME_STEP * tendency(padded_one(gas, edges))
    stepped = 0.5 * gas + 0.5 * (section_one + TIME_STEP * tendency(padded_one(section_one, edges)))
    slots = parcels.shape[0]
    move_cap = slots // 4
    raveled_vapour_state = stepped.reshape(6, -1)
    flat_bins = home_cell_index.reshape(-1)
    transported = jnp.take(raveled_vapour_state, flat_bins, axis=1).reshape(6, slots, 128)
    updated, sources = parcel_update(parcels, transported)
    own_order = order[0]
    kept = counts[0, 0]
    forward = counts[0, 1]
    backward = counts[0, 2]
    slot_ids = jnp.arange(slots, dtype=jnp.int32)
    positions = jnp.zeros((slots,), jnp.int32).at[own_order].set(slot_ids)
    live = (positions < kept + forward + backward).astype(jnp.float32)
    sources = sources * live[None, :, None]
    gas_out = (
        raveled_vapour_state.at[:, flat_bins].add(sources.reshape(6, -1)).reshape(stepped.shape)
    )
    ordered = jnp.take(updated, own_order, axis=0)
    move_ids = jnp.arange(move_cap, dtype=jnp.int32)
    front_rows = lax.dynamic_slice_in_dim(ordered, kept, move_cap, 0)
    front_rows = jnp.where((move_ids < forward)[:, None, None], front_rows, 0.0)
    back_rows = lax.dynamic_slice_in_dim(ordered, kept + forward, move_cap, 0)
    back_rows = jnp.where((move_ids < backward)[:, None, None], back_rows, 0.0)
    front_count = jnp.full((1,), forward, jnp.int32).astype(jnp.float32)
    back_count = jnp.full((1,), backward, jnp.int32).astype(jnp.float32)
    got_lower, lower_count = from_behind((front_rows, front_count), "gx", 1)
    got_upper, upper_count = from_behind((back_rows, back_count), "gx", -1)
    from_lower = lower_count[0].astype(jnp.int32)
    from_upper = upper_count[0].astype(jnp.int32)
    combined = jnp.concatenate([ordered, got_lower, got_upper], axis=0)
    in_own = slot_ids < kept
    in_lower = (slot_ids >= kept) & (slot_ids < kept + from_lower)
    in_upper = (slot_ids >= kept + from_lower) & (slot_ids < kept + from_lower + from_upper)
    source_row = jnp.where(
        in_own,
        slot_ids,
        jnp.where(
            in_lower, slots + slot_ids - kept, slots + move_cap + slot_ids - kept - from_lower
        ),
    )
    source_row = jnp.clip(source_row, 0, slots + 2 * move_cap - 1)
    valid = in_own | in_lower | in_upper
    moved_parcels = jnp.where(valid[:, None, None], jnp.take(combined, source_row, axis=0), 0.0)
    return (gas_out, moved_parcels)


def solution(mesh):
    in_specs = (
        P(None, "gx", "gy", "gz"),
        P(("gx", "gy", "gz"), None, None),
        P(("gx", "gy", "gz"), None),
        P(("gx", "gy", "gz"), None),
        P(("gx", "gy", "gz"), None),
    )
    out_specs = (P(None, "gx", "gy", "gz"), P(("gx", "gy", "gz"), None, None))
    return jax.shard_map(body, mesh=mesh, in_specs=in_specs, out_specs=out_specs, check_vma=False)
```

profile of v0, /device:TPU:27, one launch (start us, length us, event | category | flops | bytes accessed | tf_op | source)
XLA Modules:
  0.0 211.0 jit_solution(8339095322424253152)
XLA Ops:
  0.6 1.4 fusion.125
  2.6 11.3 %collective-permute-start.13 = (f32[1]{0:T(128)}, f32[1]{0:T(128)}, u32[]{:S(2)}, u32[]{:S(2)}) collective-permute-start(f32[1]{0:T(128)} %bitcast.73), channel_id=1, source_target_pairs={{32,0},{64,32},{96,64},{128,96},{160,128},{192,160},{224,192},{256... | collective-permute-start | bytes 20 | tf_op jit(solution)/shard_map/ppermute | solution.py:37
  14.5 2.6 %collective-permute-start.12 = (f32[1]{0:T(128)}, f32[1]{0:T(128)}, u32[]{:S(2)}, u32[]{:S(2)}) collective-permute-start(f32[1]{0:T(128)} %bitcast.71), channel_id=1, source_target_pairs={{0,32},{32,64},{64,96},{96,128},{128,160},{160,192},{192,224},{224... | collective-permute-start | bytes 20 | tf_op jit(solution)/shard_map/ppermute | solution.py:37
  17.9 5.5 %collective-permute-start.1 = (f32[6,1,8,128]{3,2,1,0:T(8,128)S(1)}, f32[6,1,8,128]{3,2,1,0:T(8,128)S(1)}, u32[]{:S(2)}, u32[]{:S(2)}) collective-permute-start(f32[6,1,8,128]{3,2,1,0:T(8,128)S(1)} %get-tuple-element.151), channel_id=1, source_target_pairs={{32,0},{64,32},{96,64},{128,96},{160,128},{192,160},{224,192},{256... | collective-permute-start | bytes 73736 | tf_op jit(solution)/shard_map/ppermute | solution.py:27
  23.4 1.9 collective-permute-start
  31.8 0.9 constant_dynamic-update-slice_fusion.1
  32.8 6.6 %collective-permute-start.2 = (f32[6,10,1,128]{3,2,1,0:T(1,128)S(1)}, f32[6,10,1,128]{3,2,1,0:T(1,128)S(1)}, u32[]{:S(2)}, u32[]{:S(2)}) collective-permute-start(f32[6,10,1,128]{3,2,1,0:T(1,128)S(1)} %get-tuple-element.147), channel_id=1, source_target_pairs={{0,8},{8,16},{16,24},{1,9},{9,17},{17,25},{2,10},{10,18},{18,26},{... | collective-permute-start | bytes 92168 | tf_op jit(solution)/shard_map/ppermute | solution.py:25
  39.4 1.9 collective-permute-start.3
  42.0 4.1 %collective-permute-done.3 = f32[6,10,1,128]{3,2,1,0:T(1,128)S(1)} collective-permute-done((f32[6,10,1,128]{3,2,1,0:T(1,128)S(1)}, f32[6,10,1,128]{3,2,1,0:T(1,128)S(1)}, u32[]{:S(2)}, u32[]{:S(2)}) %collective-permute-start.3) | collective-permute-done | bytes 30752 | tf_op jit(solution)/shard_map/ppermute | solution.py:27
  46.4 4.4 %collective-permute-start.4 = (f32[6,10,10,1]{3,2,1,0:T(8,128)S(1)}, f32[6,10,10,1]{3,2,1,0:T(8,128)S(1)}, u32[]{:S(2)}, u32[]{:S(2)}) collective-permute-start(f32[6,10,10,1]{3,2,1,0:T(8,128)S(1)} %get-tuple-element.136), channel_id=1, source_target_pairs={{0,1},{1,2},{2,3},{3,4},{4,5},{5,6},{6,7},{8,9},{9,10},{10,11},{11... | collective-permute-start | bytes 7208 | tf_op jit(solution)/shard_map/ppermute | solution.py:25
  50.8 1.9 collective-permute-start.5
  56.5 2.2 %collective-permute-done.4 = f32[6,10,10,1]{3,2,1,0:T(8,128)S(1)} collective-permute-done((f32[6,10,10,1]{3,2,1,0:T(8,128)S(1)}, f32[6,10,10,1]{3,2,1,0:T(8,128)S(1)}, u32[]{:S(2)}, u32[]{:S(2)}) %collective-permute-start.4) | collective-permute-done | bytes 2432 | tf_op jit(solution)/shard_map/ppermute | solution.py:25
  58.7 5.3 %collective-permute-done.5 = f32[6,10,10,1]{3,2,1,0:T(8,128)S(1)} collective-permute-done((f32[6,10,10,1]{3,2,1,0:T(8,128)S(1)}, f32[6,10,10,1]{3,2,1,0:T(8,128)S(1)}, u32[]{:S(2)}, u32[]{:S(2)}) %collective-permute-start.5) | collective-permute-done | bytes 2432 | tf_op jit(solution)/shard_map/ppermute | solution.py:27
  67.9 1.0 select_select_fusion.3
  71.9 1.9 collective-permute-start.6
  73.8 6.4 %collective-permute-start.7 = (f32[6,1,8,128]{3,2,1,0:T(8,128)S(1)}, f32[6,1,8,128]{3,2,1,0:T(8,128)S(1)}, u32[]{:S(2)}, u32[]{:S(2)}) collective-permute-start(f32[6,1,8,128]{3,2,1,0:T(8,128)S(1)} %get-tuple-element.150), channel_id=1, source_target_pairs={{32,0},{64,32},{96,64},{128,96},{160,128},{192,160},{224,192},{256... | collective-permute-start | bytes 73736 | tf_op jit(solution)/shard_map/ppermute | solution.py:27
  81.2 1.9 collective-permute-start.8
  83.1 2.4 %collective-permute-start.9 = (f32[6,10,1,128]{3,2,1,0:T(1,128)S(1)}, f32[6,10,1,128]{3,2,1,0:T(1,128)S(1)}, u32[]{:S(2)}, u32[]{:S(2)}) collective-permute-start(f32[6,10,1,128]{3,2,1,0:T(1,128)S(1)} %get-tuple-element.146), channel_id=1, source_target_pairs={{8,0},{16,8},{24,16},{9,1},{17,9},{25,17},{10,2},{18,10},{26,18},{... | collective-permute-start | bytes 92168 | tf_op jit(solution)/shard_map/ppermute | solution.py:27
  86.2 3.6 %collective-permute-done.9 = f32[6,10,1,128]{3,2,1,0:T(1,128)S(1)} collective-permute-done((f32[6,10,1,128]{3,2,1,0:T(1,128)S(1)}, f32[6,10,1,128]{3,2,1,0:T(1,128)S(1)}, u32[]{:S(2)}, u32[]{:S(2)}) %collective-permute-start.9) | collective-permute-done | bytes 30752 | tf_op jit(solution)/shard_map/ppermute | solution.py:27
  90.1 1.9 collective-permute-start.10
  92.0 3.5 %collective-permute-start.11 = (f32[6,10,10,1]{3,2,1,0:T(8,128)S(1)}, f32[6,10,10,1]{3,2,1,0:T(8,128)S(1)}, u32[]{:S(2)}, u32[]{:S(2)}) collective-permute-start(f32[6,10,10,1]{3,2,1,0:T(8,128)S(1)} %get-tuple-element.135), channel_id=1, source_target_pairs={{1,0},{2,1},{3,2},{4,3},{5,4},{6,5},{7,6},{9,8},{10,9},{11,10},{12... | collective-permute-start | bytes 7208 | tf_op jit(solution)/shard_map/ppermute | solution.py:27
  96.3 6.3 %collective-permute-done.10 = f32[6,10,10,1]{3,2,1,0:T(8,128)S(1)} collective-permute-done((f32[6,10,10,1]{3,2,1,0:T(8,128)S(1)}, f32[6,10,10,1]{3,2,1,0:T(8,128)S(1)}, u32[]{:S(2)}, u32[]{:S(2)}) %collective-permute-start.10) | collective-permute-done | bytes 2432 | tf_op jit(solution)/shard_map/ppermute | solution.py:25
  102.6 2.8 %collective-permute-done.11 = f32[6,10,10,1]{3,2,1,0:T(8,128)S(1)} collective-permute-done((f32[6,10,10,1]{3,2,1,0:T(8,128)S(1)}, f32[6,10,10,1]{3,2,1,0:T(8,128)S(1)}, u32[]{:S(2)}, u32[]{:S(2)}) %collective-permute-start.11) | collective-permute-done | bytes 2432 | tf_op jit(solution)/shard_map/ppermute | solution.py:27
  109.3 1.0 select_select_fusion
  113.3 2.7 %copy.1355 = f32[6,8,8,128]{0,3,2,1:T(8,128)} copy(f32[6,8,8,128]{3,2,1,0:T(8,128)S(1)} %add_multiply_fusion) | data formatting | bytes 393216 | tf_op jit(solution)/shard_map/reshape | solution.py:160
  116.0 30.2 %gather_fusion = f32[8192,6]{1,0:T(8,128)} fusion(f32[6,8192]{0,1:T(8,128)} %bitcast.345, s32[8192]{0:T(1024)S(1)} %broadcast_clamp_fusion), kind=kCustom, calls=%fused_computation | custom fusion | bytes 425984 | tf_op jit(solution)/shard_map/jit(_take)/gather | solution.py:162
  146.2 2.8 %copy.1341 = f32[8192,6]{0,1:T(8,128)S(1)} copy(f32[8192,6]{1,0:T(8,128)} %gather_fusion) | data formatting | bytes 393216 | tf_op jit(solution)/shard_map/jit(_take)/gather | solution.py:162
  151.1 1.9 collective-permute-start.14
  153.0 6.0 %collective-permute-start.15 = (f32[16,5,128]{2,1,0:T(8,128)S(1)}, f32[16,5,128]{2,1,0:T(8,128)S(1)}, u32[]{:S(2)}, u32[]{:S(2)}) collective-permute-start(f32[16,5,128]{2,1,0:T(8,128)S(1)} %get-tuple-element.139), channel_id=1, source_target_pairs={{32,0},{64,32},{96,64},{128,96},{160,128},{192,160},{224,192},{256... | collective-permute-start | bytes 122888 | tf_op jit(solution)/shard_map/ppermute | solution.py:37
  159.1 2.7 %copy.1343 = f32[8192,6]{1,0:T(8,128)} copy(f32[8192,6]{0,1:T(8,128)S(1)} %fusion.12) | data formatting | bytes 393216 | tf_op jit(solution)/shard_map/mul | solution.py:171
  161.9 44.0 %scatter_fusion = f32[6,8192]{0,1:T(8,128)} fusion(f32[6,8192]{0,1:T(8,128)} %bitcast.346, s32[8192]{0:T(1024)S(1)} %bitcast.368, f32[8192,6]{1,0:T(8,128)} %copy.1343), kind=kCustom, calls=%fused_computation.4 | custom fusion | flops 49152 | bytes 622592 | tf_op jit(solution)/shard_map/scatter-add | solution.py:173
  205.9 3.5 %copy.1345 = f32[6,8,8,128]{3,2,1,0:T(8,128)} copy(f32[6,8,8,128]{0,3,2,1:T(8,128)} %bitcast.347) | data formatting | bytes 393216
  (150 shorter events, 25.7 us)
Async XLA Ops:
  2.6 82.9 %collective-permute-start.13 = (f32[1]{0:T(128)}, f32[1]{0:T(128)}, u32[]{:S(2)}, u32[]{:S(2)}) collective-permute-start(f32[1]{0:T(128)} %bitcast.73), channel_id=1, source_target_pairs={{32,0},{64,32},{96,64},{128,96},{160,128},{192,160},{224,192},{256... | collective-permute-start | bytes 20 | tf_op jit(solution)/shard_map/ppermute | solution.py:37
  14.5 40.7 %collective-permute-start.12 = (f32[1]{0:T(128)}, f32[1]{0:T(128)}, u32[]{:S(2)}, u32[]{:S(2)}) collective-permute-start(f32[1]{0:T(128)} %bitcast.71), channel_id=1, source_target_pairs={{0,32},{32,64},{64,96},{96,128},{128,160},{160,192},{192,224},{224... | collective-permute-start | bytes 20 | tf_op jit(solution)/shard_map/ppermute | solution.py:37
  17.9 14.8 %collective-permute-start.1 = (f32[6,1,8,128]{3,2,1,0:T(8,128)S(1)}, f32[6,1,8,128]{3,2,1,0:T(8,128)S(1)}, u32[]{:S(2)}, u32[]{:S(2)}) collective-permute-start(f32[6,1,8,128]{3,2,1,0:T(8,128)S(1)} %get-tuple-element.151), channel_id=1, source_target_pairs={{32,0},{64,32},{96,64},{128,96},{160,128},{192,160},{224,192},{256... | collective-permute-start | bytes 73736 | tf_op jit(solution)/shard_map/ppermute | solution.py:27
  23.4 8.4 %collective-permute-start = (f32[6,1,8,128]{3,2,1,0:T(8,128)S(1)}, f32[6,1,8,128]{3,2,1,0:T(8,128)S(1)}, u32[]{:S(2)}, u32[]{:S(2)}) collective-permute-start(f32[6,1,8,128]{3,2,1,0:T(8,128)S(1)} %get-tuple-element.152), channel_id=1, source_target_pairs={{0,32},{32,64},{64,96},{96,128},{128,160},{160,192},{192,224},{224... | collective-permute-start | bytes 73736 | tf_op jit(solution)/shard_map/ppermute | solution.py:25
  32.8 9.2 %collective-permute-start.2 = (f32[6,10,1,128]{3,2,1,0:T(1,128)S(1)}, f32[6,10,1,128]{3,2,1,0:T(1,128)S(1)}, u32[]{:S(2)}, u32[]{:S(2)}) collective-permute-start(f32[6,10,1,128]{3,2,1,0:T(1,128)S(1)} %get-tuple-element.147), channel_id=1, source_target_pairs={{0,8},{8,16},{16,24},{1,9},{9,17},{17,25},{2,10},{10,18},{18,26},{... | collective-permute-start | bytes 92168 | tf_op jit(solution)/shard_map/ppermute | solution.py:25
  39.4 6.7 %collective-permute-start.3 = (f32[6,10,1,128]{3,2,1,0:T(1,128)S(1)}, f32[6,10,1,128]{3,2,1,0:T(1,128)S(1)}, u32[]{:S(2)}, u32[]{:S(2)}) collective-permute-start(f32[6,10,1,128]{3,2,1,0:T(1,128)S(1)} %get-tuple-element.148), channel_id=1, source_target_pairs={{8,0},{16,8},{24,16},{9,1},{17,9},{25,17},{10,2},{18,10},{26,18},{... | collective-permute-start | bytes 92168 | tf_op jit(solution)/shard_map/ppermute | solution.py:27
  46.4 12.3 %collective-permute-start.4 = (f32[6,10,10,1]{3,2,1,0:T(8,128)S(1)}, f32[6,10,10,1]{3,2,1,0:T(8,128)S(1)}, u32[]{:S(2)}, u32[]{:S(2)}) collective-permute-start(f32[6,10,10,1]{3,2,1,0:T(8,128)S(1)} %get-tuple-element.136), channel_id=1, source_target_pairs={{0,1},{1,2},{2,3},{3,4},{4,5},{5,6},{6,7},{8,9},{9,10},{10,11},{11... | collective-permute-start | bytes 7208 | tf_op jit(solution)/shard_map/ppermute | solution.py:25
  50.8 13.2 %collective-permute-start.5 = (f32[6,10,10,1]{3,2,1,0:T(8,128)S(1)}, f32[6,10,10,1]{3,2,1,0:T(8,128)S(1)}, u32[]{:S(2)}, u32[]{:S(2)}) collective-permute-start(f32[6,10,10,1]{3,2,1,0:T(8,128)S(1)} %get-tuple-element.137), channel_id=1, source_target_pairs={{1,0},{2,1},{3,2},{4,3},{5,4},{6,5},{7,6},{9,8},{10,9},{11,10},{12... | collective-permute-start | bytes 7208 | tf_op jit(solution)/shard_map/ppermute | solution.py:27
  70.5 1.4 copy-start
  71.9 9.0 %collective-permute-start.6 = (f32[6,1,8,128]{3,2,1,0:T(8,128)S(1)}, f32[6,1,8,128]{3,2,1,0:T(8,128)S(1)}, u32[]{:S(2)}, u32[]{:S(2)}) collective-permute-start(f32[6,1,8,128]{3,2,1,0:T(8,128)S(1)} %get-tuple-element.149), channel_id=1, source_target_pairs={{0,32},{32,64},{64,96},{96,128},{128,160},{160,192},{192,224},{224... | collective-permute-start | bytes 73736 | tf_op jit(solution)/shard_map/ppermute | solution.py:25
  73.8 7.3 %collective-permute-start.7 = (f32[6,1,8,128]{3,2,1,0:T(8,128)S(1)}, f32[6,1,8,128]{3,2,1,0:T(8,128)S(1)}, u32[]{:S(2)}, u32[]{:S(2)}) collective-permute-start(f32[6,1,8,128]{3,2,1,0:T(8,128)S(1)} %get-tuple-element.150), channel_id=1, source_target_pairs={{32,0},{64,32},{96,64},{128,96},{160,128},{192,160},{224,192},{256... | collective-permute-start | bytes 73736 | tf_op jit(solution)/shard_map/ppermute | solution.py:27
  81.2 5.0 %collective-permute-start.8 = (f32[6,10,1,128]{3,2,1,0:T(1,128)S(1)}, f32[6,10,1,128]{3,2,1,0:T(1,128)S(1)}, u32[]{:S(2)}, u32[]{:S(2)}) collective-permute-start(f32[6,10,1,128]{3,2,1,0:T(1,128)S(1)} %get-tuple-element.145), channel_id=1, source_target_pairs={{0,8},{8,16},{16,24},{1,9},{9,17},{17,25},{2,10},{10,18},{18,26},{... | collective-permute-start | bytes 92168 | tf_op jit(solution)/shard_map/ppermute | solution.py:25
  83.1 6.7 %collective-permute-start.9 = (f32[6,10,1,128]{3,2,1,0:T(1,128)S(1)}, f32[6,10,1,128]{3,2,1,0:T(1,128)S(1)}, u32[]{:S(2)}, u32[]{:S(2)}) collective-permute-start(f32[6,10,1,128]{3,2,1,0:T(1,128)S(1)} %get-tuple-element.146), channel_id=1, source_target_pairs={{8,0},{16,8},{24,16},{9,1},{17,9},{25,17},{10,2},{18,10},{26,18},{... | collective-permute-start | bytes 92168 | tf_op jit(solution)/shard_map/ppermute | solution.py:27
  90.1 12.5 %collective-permute-start.10 = (f32[6,10,10,1]{3,2,1,0:T(8,128)S(1)}, f32[6,10,10,1]{3,2,1,0:T(8,128)S(1)}, u32[]{:S(2)}, u32[]{:S(2)}) collective-permute-start(f32[6,10,10,1]{3,2,1,0:T(8,128)S(1)} %get-tuple-element.134), channel_id=1, source_target_pairs={{0,1},{1,2},{2,3},{3,4},{4,5},{5,6},{6,7},{8,9},{9,10},{10,11},{11... | collective-permute-start | bytes 7208 | tf_op jit(solution)/shard_map/ppermute | solution.py:25
  92.0 13.4 %collective-permute-start.11 = (f32[6,10,10,1]{3,2,1,0:T(8,128)S(1)}, f32[6,10,10,1]{3,2,1,0:T(8,128)S(1)}, u32[]{:S(2)}, u32[]{:S(2)}) collective-permute-start(f32[6,10,10,1]{3,2,1,0:T(8,128)S(1)} %get-tuple-element.135), channel_id=1, source_target_pairs={{1,0},{2,1},{3,2},{4,3},{5,4},{6,5},{7,6},{9,8},{10,9},{11,10},{12... | collective-permute-start | bytes 7208 | tf_op jit(solution)/shard_map/ppermute | solution.py:27
  116.0 33.3 %copy-start.1 = (f32[64,5,128]{2,0,1:T(8,128)S(1)}, f32[64,5,128]{2,0,1:T(8,128)}, u32[]{:S(2)}) copy-start(f32[64,5,128]{2,0,1:T(8,128)} %param.14) | copy-start | bytes 491524
  151.1 58.3 %collective-permute-start.14 = (f32[16,5,128]{2,1,0:T(8,128)S(1)}, f32[16,5,128]{2,1,0:T(8,128)S(1)}, u32[]{:S(2)}, u32[]{:S(2)}) collective-permute-start(f32[16,5,128]{2,1,0:T(8,128)S(1)} %get-tuple-element.138), channel_id=1, source_target_pairs={{0,32},{32,64},{64,96},{96,128},{128,160},{160,192},{192,224},{224... | collective-permute-start | bytes 122888 | tf_op jit(solution)/shard_map/ppermute | solution.py:37
  153.0 56.4 %collective-permute-start.15 = (f32[16,5,128]{2,1,0:T(8,128)S(1)}, f32[16,5,128]{2,1,0:T(8,128)S(1)}, u32[]{:S(2)}, u32[]{:S(2)}) collective-permute-start(f32[16,5,128]{2,1,0:T(8,128)S(1)} %get-tuple-element.139), channel_id=1, source_target_pairs={{32,0},{64,32},{96,64},{128,96},{160,128},{192,160},{224,192},{256... | collective-permute-start | bytes 122888 | tf_op jit(solution)/shard_map/ppermute | solution.py:37
where the time goes:
time: 212 us; the launch traced here: 211 us
  other arithmetic  62.7 us (30%)
  starting transfers between devices  62.2 us (29%)
  local copies, waits for them, and re-layouts  52.9 us (25%)
  waiting for transfers between devices  24.8 us (12%)
  between operations  8.38 us (4%)
    scatter-add x1, other arithmetic, body(): raveled_vapour_state.at[:, flat_bins].add(sources.reshape(6, -1))  44 us
    gather x2, local copies, waits for them, and re-layouts, body(): jnp.take(raveled_vapour_state, flat_bins, axis=1).reshape(6, slots, 128)  33 us
    ppermute x4, starting transfers between devices, from_behind(): return lax.ppermute(block, axis, route)  21.9 us
    ppermute x6, starting transfers between devices, padded_2(): lax.ppermute(head, axis, [((i + 1) % count, i) for i in range(ends)])  21.6 us
    ppermute x6, starting transfers between devices, padded_2(): lax.ppermute(tail, axis, [(i, (i + 1) % count) for i in range(ends)])  18.7 us
    ppermute x6, waiting for transfers between devices, padded_2(): lax.ppermute(head, axis, [((i + 1) % count, i) for i in range(ends)])  16.2 us
    ppermute x6, waiting for transfers between devices, padded_2(): lax.ppermute(tail, axis, [(i, (i + 1) % count) for i in range(ends)])  8.57 us
    unnamed x19, local copies, waits for them, and re-layouts  5.62 us
  transfers between devices with their start and end apart: 16, of which 7 were waited for; matrix products, arithmetic and copies ran while one was open for 32% of the time, Pallas kernels for 0%

commit v1 on v0

v1 whole, which is shorter than its diff:
```python
import jax
import jax.numpy as jnp
from jax import lax
from jax.experimental import pallas as pl
from jax.experimental.pallas import tpu as pltpu
from jax.sharding import PartitionSpec as P

GAMMA = 1.4
TIME_STEP = 0.1
RATE = 3.0
ACTIVATION = 2.0
HEAT = 5.0
DRAG_RELAX_TIME = 0.4
HEATING_RELAX = 0.6
EVAP_RATE = 1.5
LIQUID_HEAT = 2.0

F32 = jnp.float32
BF16 = jnp.bfloat16
INTERPRET = False


def shifted(block, axis, step):
    count = lax.axis_size(axis)
    return lax.ppermute(block, axis, [(i, i + step) for i in range(count) if 0 <= i + step < count])


def ends(axis):
    at = lax.axis_index(axis)
    return at == 0, at == lax.axis_size(axis) - 1


def call(kernel, outs, **kwargs):
    return pl.pallas_call(
        kernel,
        out_shape=[jax.ShapeDtypeStruct(shape, F32) for shape in outs],
        interpret=INTERPRET,
        **kwargs,
    )


def sublane(shape):
    return lax.broadcasted_iota(jnp.int32, shape, len(shape) - 2)


def lane(shape):
    return lax.broadcasted_iota(jnp.int32, shape, len(shape) - 1)


def turn(v, shift, axis):
    size = v.shape[axis]
    shift %= size
    return v if shift == 0 else pltpu.roll(v, shift, axis)


def pack_y(gas, xlo, xhi, rows, low_pay, high_pay):
    first, last = ends("gx")
    sub = sublane((8, 128))
    for c in range(6):
        line = []
        for i in range(12):
            if i < 2:
                line.append(jnp.where(first, gas[c, 0], xlo[c, i]))
                rows[c, i] = line[-1]
            elif i < 10:
                line.append(gas[c, i - 2])
            else:
                line.append(jnp.where(last, gas[c, 7], xhi[c, i - 10]))
                rows[c, i - 8] = line[-1]
        for g in range(3):
            low = line[4 * g]
            high = turn(line[4 * g], 2, 0)
            for k in range(1, 4):
                here = (sub >= 2 * k) & (sub < 2 * k + 2)
                low = jnp.where(here, turn(line[4 * g + k], 2 * k, 0), low)
                high = jnp.where(here, turn(line[4 * g + k], 2 * k + 2, 0), high)
            low_pay[c, g] = low
            high_pay[c, g] = high


def pack_z(gas, rows, ylo, yhi, box, pay):
    first, last = ends("gy")
    sub = sublane((8, 128))
    group = lane((16, 128)) // 8
    for c in range(6):
        packed = None
        for i in range(12):
            if 2 <= i < 10:
                mid = gas[c, i - 2]
            else:
                mid = rows[c, i if i < 2 else i - 8]
            g, k = i // 4, i % 4
            below = turn(ylo[c, g], 6 - 2 * k, 0)
            above = turn(yhi[c, g], -2 * k, 0)
            below = jnp.where(first, jnp.broadcast_to(mid[0:1], (8, 128)), below)
            above = jnp.where(last, jnp.broadcast_to(mid[7:8], (8, 128)), above)
            line = jnp.concatenate([mid, jnp.where(sub < 4, above, below)], axis=0)
            box[c, i] = line
            moved = turn(line, 8 * i + 2, 1)
            packed = moved if packed is None else jnp.where(group == i, moved, packed)
        pay[c] = packed


def primitives(state):
    r, m1, m2, m3, e, _ = state
    inv = 1.0 / r
    u = (m1 * inv, m2 * inv, m3 * inv)
    p = (GAMMA - 1.0) * (e - 0.5 * (m1 * u[0] + m2 * u[1] + m3 * u[2]))
    return u, p, jnp.sqrt(GAMMA * p * inv)


def along(state, prim, k):
    u, p, sound = prim
    uk = u[k]
    flux = [state[1 + k], state[1] * uk, state[2] * uk, state[3] * uk, (state[4] + p) * uk, state[5] * uk]
    flux[1 + k] = flux[1 + k] + p
    return flux, jnp.abs(uk) + sound, state


def face(lower, upper):
    speed = jnp.maximum(lower[1], upper[1])
    return [
        (fa + fb) - speed * (b - a)
        for fa, fb, a, b in zip(lower[0], upper[0], lower[2], upper[2], strict=True)
    ]


def over(part, move):
    flux, speed, state = part
    return [move(f) for f in flux], move(speed), [move(v) for v in state]


def advanced(state, prim, total):
    burned = RATE * state[5] * jnp.exp(-ACTIVATION * state[0] / prim[1])
    out = [v - (0.5 * TIME_STEP) * t for v, t in zip(state, total, strict=True)]
    out[4] = out[4] + (TIME_STEP * HEAT) * burned
    out[5] = out[5] - TIME_STEP * burned
    return out


def cyclic_net(state, prim, k, distance, axis):
    part = along(state, prim, k)
    faces = face(part, over(part, lambda v: turn(v, -distance, axis)))
    return faces, [f - turn(f, distance, axis) for f in faces]


def side_state(own, below, above, first, last):
    at = lane((16, 128)) % 8
    low = jnp.where(at < 2, jnp.where(first, jnp.where(at == 0, turn(own, -2, 1), turn(own, -1, 1)), below), own)
    high = jnp.where(at < 2, own, jnp.where(last, jnp.where(at == 2, turn(own, 1, 1), turn(own, 2, 1)), above))
    return jnp.where(at < 4, low, turn(high, 4, 1))


def side_inflow(faces):
    at = lane((16, 128)) % 8
    return [jnp.where(at == 0, turn(f, -5, 1), -f) for f in faces]


def closed_net(part, inflow, i):
    at = lane(part[1].shape)
    faces = face(part, over(part, lambda v: turn(v, -1, 1)))
    net = []
    for f, s in zip(faces, inflow, strict=True):
        f = jnp.where(at == 127, 0.0, f)
        outer = turn(s[: f.shape[0]], 127 - 8 * i, 1)
        net.append(f - turn(f, 1, 1) + jnp.where((at == 0) | (at == 127), outer, 0.0))
    return net


def gas_step(box, own, below, above, stepped, ahead):
    first_x, last_x = ends("gx")
    first_y, last_y = ends("gy")
    first_z, last_z = ends("gz")
    sub = sublane((16, 128))
    at = lane((16, 128)) % 8
    group = lane((16, 128)) // 8

    def clamp_y(v):
        v = jnp.where(first_y & (sub == 15), jnp.broadcast_to(v[0:1], v.shape), v)
        return jnp.where(last_y & (sub == 8), jnp.broadcast_to(v[7:8], v.shape), v)

    def clamp_x_z(v):
        v = jnp.where(first_x & (group == 1), turn(v, -8, 1), v)
        v = jnp.where(last_x & (group == 10), turn(v, 8, 1), v)
        v = jnp.where(first_z & (at == 1), turn(v, -1, 1), v)
        return jnp.where(last_z & (at == 6), turn(v, 1, 1), v)

    side = [side_state(own[c], below[c], above[c], first_z, last_z) for c in range(6)]
    prim = primitives(side)
    faces, net_z = cyclic_net(side, prim, 2, 1, 1)
    inflow_one = side_inflow(faces)
    _, net_x = cyclic_net(side, prim, 0, 8, 1)
    _, net_y = cyclic_net(side, prim, 1, 1, 0)
    side = advanced(side, prim, [x + y + z for x, y, z in zip(net_x, net_y, net_z, strict=True)])
    side = [clamp_y(clamp_x_z(v)) for v in side]
    inflow_two = side_inflow(cyclic_net(side, primitives(side), 2, 1, 1)[0])

    state = [box[c, 0] for c in range(6)]
    part = along(state, primitives(state), 0)
    state = [box[c, 1] for c in range(6)]
    prim = primitives(state)
    next_part = along(state, prim, 0)
    faces = face(part, next_part)
    for i in range(1, 11):
        part = next_part
        next_state = [box[c, i + 1] for c in range(6)]
        next_prim = primitives(next_state)
        next_part = along(next_state, next_prim, 0)
        next_faces = face(part, next_part)
        _, net_y = cyclic_net(state, prim, 1, 1, 0)
        net_z = closed_net(along(state, prim, 2), inflow_one, i)
        total = [b - a + y + z for a, b, y, z in zip(faces, next_faces, net_y, net_z, strict=True)]
        for c, v in enumerate(advanced(state, prim, total)):
            ahead[c, i] = clamp_y(v)
        state, prim, faces = next_state, next_prim, next_faces

    def row(i):
        v = [ahead[c, i] for c in range(6)]
        if i == 1:
            v = [jnp.where(first_x, ahead[c, 2], v[c]) for c in range(6)]
        if i == 10:
            v = [jnp.where(last_x, ahead[c, 9], v[c]) for c in range(6)]
        return v

    def inner(values):
        return [v[:8] for v in values]

    def inner_prim(prim):
        return inner(prim[0]), prim[1][:8], prim[2][:8]

    state = inner(row(1))
    part = along(state, primitives(state), 0)
    full = row(2)
    full_prim = primitives(full)
    state, prim = inner(full), inner_prim(full_prim)
    next_part = along(state, prim, 0)
    faces = face(part, next_part)
    for i in range(2, 10):
        part = next_part
        next_full = row(i + 1)
        next_full_prim = primitives(next_full)
        next_state, next_prim = inner(next_full), inner_prim(next_full_prim)
        next_part = along(next_state, next_prim, 0)
        next_faces = face(part, next_part)
        _, net_y = cyclic_net(full, full_prim, 1, 1, 0)
        net_z = closed_net(along(state, prim, 2), inflow_two, i)
        total = [b - a + y[:8] + z for a, b, y, z in zip(faces, next_faces, net_y, net_z, strict=True)]
        for c, v in enumerate(advanced(state, prim, total)):
            stepped[c, i - 2] = 0.5 * box[c, i, 0:8] + 0.5 * v
        full, full_prim, state, prim, faces = next_full, next_full_prim, next_state, next_prim, next_faces


def two_parts(v):
    big = v.astype(BF16)
    return big, (v - big.astype(F32)).astype(BF16)


def split_cell(cells):
    return (cells >> 7) & 31, ((cells >> 12) << 7) | (cells & 127)


def one_hot(index, count):
    return jnp.where(sublane((count, index.shape[-1])) == index, 1.0, 0.0)


def gather_update(order, counts, box, own, below, above, parcels, cells, stepped, sources, updated, front, back, ahead, table, carried, live):
    gas_step(box, own, below, above, stepped, ahead)

    for c in range(6):
        left, right = (jnp.reshape(stepped[c, x : x + 4], (32, 128)) for x in (0, 4))
        big, small = two_parts(jnp.concatenate([left, right], axis=1))
        table[pl.ds(32 * c, 32), :] = big
        table[pl.ds(192 + 32 * c, 32), :] = small

    def chunk(n, _):
        index = cells[pl.ds(2 * n, 2), :]
        index = jnp.concatenate([index[0:1], index[1:2]], axis=1)
        row, column = split_cell(index)
        found = jnp.dot(table[...], one_hot(column, 256).astype(BF16), preferred_element_type=F32)
        chosen = sublane((32, 256)) == row
        for c in range(6):
            both = found[32 * c : 32 * c + 32] + found[192 + 32 * c : 224 + 32 * c]
            value = jnp.sum(jnp.where(chosen, both, 0.0), axis=0, keepdims=True)
            carried[c, pl.ds(2 * n, 1), :] = value[:, :128]
            carried[c, pl.ds(2 * n + 1, 1), :] = value[:, 128:]
        return 0

    lax.fori_loop(0, 32, chunk, 0)

    kept, forward, backward = counts[0, 0], counts[0, 1], counts[0, 2]

    def mark(j, _):
        alive = jnp.where(j < kept + forward + backward, 1.0, 0.0)
        live[pl.ds(order[0, j], 1), :] = jnp.full((1, 128), alive, F32)
        return 0

    lax.fori_loop(0, 64, mark, 0)

    r, m1, m2, m3, e, q = (carried[c] for c in range(6))
    inv = 1.0 / r
    g = (m1 * inv, m2 * inv, m3 * inv)
    t = (GAMMA - 1.0) * (e - 0.5 * (m1 * g[0] + m2 * g[1] + m3 * g[2])) * inv
    y = q * inv
    v = tuple(parcels[:, k, :] for k in range(3))
    mass, heat = parcels[:, 3, :], parcels[:, 4, :]
    root = jnp.sqrt(mass)
    inv_root = 1.0 / root
    new_mass = mass * jnp.exp(-TIME_STEP * EVAP_RATE * t / (root * (1.0 + y * y)))
    slow = jnp.exp((-TIME_STEP / DRAG_RELAX_TIME) * inv_root)
    new_v = tuple(gk + (vk - gk) * slow for gk, vk in zip(g, v, strict=True))
    new_heat = t + (heat - t) * jnp.exp((-TIME_STEP / HEATING_RELAX) * inv_root)
    alive = live[...]
    sources[0] = (mass - new_mass) * alive
    for k in range(3):
        sources[1 + k] = (mass * v[k] - new_mass * new_v[k]) * alive
    square = v[0] * v[0] + v[1] * v[1] + v[2] * v[2]
    new_square = new_v[0] * new_v[0] + new_v[1] * new_v[1] + new_v[2] * new_v[2]
    sources[4] = (
        0.5 * (mass * square - new_mass * new_square) + LIQUID_HEAT * (mass * heat - new_mass * new_heat)
    ) * alive
    for k in range(3):
        updated[:, k, :] = new_v[k]
    updated[:, 3, :] = new_mass
    updated[:, 4, :] = new_heat
    for k in range(5, 8):
        updated[:, k, :] = jnp.zeros((64, 128), F32)

    row_five = sublane((8, 128)) == 5
    for out, start, size in ((front, kept, forward), (back, kept + forward, backward)):

        def send(j, _, out=out, start=start, size=size):
            block = updated[order[0, jnp.minimum(start + j, 63)]]
            out[j] = jnp.where(row_five, size.astype(F32), block)
            return 0

        lax.fori_loop(0, 16, send, 0)


def scatter(stepped, sources, cells, gas_out):
    total = None
    for n in range(8):
        columns, big, small = [], [], []
        for b in range(8 * n, 8 * n + 8):
            row, column = split_cell(cells[b : b + 1, :])
            columns.append(one_hot(column, 256).astype(BF16))
            chosen = sublane((32, 128)) == row
            wide = [
                jnp.where(chosen, jnp.broadcast_to(sources[c, b : b + 1, :], (32, 128)), 0.0) for c in range(5)
            ]
            wide = two_parts(jnp.concatenate(wide, axis=0))
            big.append(wide[0])
            small.append(wide[1])
        left = jnp.concatenate([jnp.concatenate(big, axis=1), jnp.concatenate(small, axis=1)], axis=0)
        part = lax.dot_general(
            left, jnp.concatenate(columns, axis=1), (((1,), (1,)), ((), ())), preferred_element_type=F32
        )
        total = part if total is None else total + part
    for c in range(6):
        k = c % 5
        both = total[32 * k : 32 * k + 32] + total[160 + 32 * k : 192 + 32 * k]
        for half in range(2):
            added = jnp.reshape(both[:, 128 * half : 128 * half + 128], (4, 8, 128))
            gas_out[c, 4 * half : 4 * half + 4] = stepped[c, 4 * half : 4 * half + 4] + added


def place(order, counts, updated, lower, upper, moved):
    kept = counts[0, 0]
    has_lower = jnp.logical_not(ends("gx")[0])
    has_upper = jnp.logical_not(ends("gx")[1])
    from_lower = jnp.where(has_lower, lower[0, 5, 0], 0.0).astype(jnp.int32)
    from_upper = jnp.where(has_upper, upper[0, 5, 0], 0.0).astype(jnp.int32)
    moved[...] = jnp.zeros((64, 5, 128), F32)

    def own(j, _):
        moved[j] = updated[order[0, j]][:5]
        return 0

    def low(j, _):
        moved[kept + j] = lower[j][:5]
        return 0

    def high(j, _):
        moved[kept + from_lower + j] = upper[j][:5]
        return 0

    lax.fori_loop(0, kept, own, 0)
    lax.fori_loop(0, from_lower, low, 0)
    lax.fori_loop(0, from_upper, high, 0)


def body(gas, parcels, home_cell_index, order, counts):
    smem = pl.BlockSpec(memory_space=pltpu.SMEM)
    vmem = pl.BlockSpec(memory_space=pltpu.VMEM)
    xlo = shifted(gas[:, 6:8], "gx", 1)
    xhi = shifted(gas[:, 0:2], "gx", -1)
    rows, low, high = call(pack_y, [(6, 4, 8, 128), (6, 3, 8, 128), (6, 3, 8, 128)])(gas, xlo, xhi)
    ylo = shifted(high, "gy", 1)
    yhi = shifted(low, "gy", -1)
    box, pay = call(pack_z, [(6, 12, 16, 128), (6, 16, 128)])(gas, rows, ylo, yhi)
    below = shifted(pay, "gz", 1)
    above = shifted(pay, "gz", -1)
    stepped, sources, updated, front, back = call(
        gather_update,
        [(6, 8, 8, 128), (5, 64, 128), (64, 8, 128), (16, 8, 128), (16, 8, 128)],
        in_specs=[smem, smem] + [vmem] * 6,
        scratch_shapes=[
            pltpu.VMEM((6, 12, 16, 128), F32),
            pltpu.VMEM((384, 256), BF16),
            pltpu.VMEM((6, 64, 128), F32),
            pltpu.VMEM((64, 128), F32),
        ],
    )(order, counts, box, pay, below, above, parcels, home_cell_index)
    lower = shifted(front, "gx", 1)
    upper = shifted(back, "gx", -1)
    (gas_out,) = call(scatter, [(6, 8, 8, 128)])(stepped, sources, home_cell_index)
    (moved,) = call(place, [(64, 5, 128)], in_specs=[smem, smem] + [vmem] * 3)(order, counts, updated, lower, upper)
    return gas_out, moved


def solution(mesh):
    blocks = ("gx", "gy", "gz")
    in_specs = (
        P(None, *blocks),
        P(blocks, None, None),
        P(blocks, None),
        P(blocks, None),
        P(blocks, None),
    )
    out_specs = (P(None, *blocks), P(blocks, None, None))
    return jax.shard_map(body, mesh=mesh, in_specs=in_specs, out_specs=out_specs, check_vma=False)
```

time: 212 us -> 74.5 us (0.35)
  the two profiles are of different devices: /device:TPU:27 before, /device:TPU:35 now
where the time goes in v1:
time: 74.5 us; the launch traced here: 74 us
  starting transfers between devices  33 us (44%)
  Pallas kernels  21.6 us (29%)
  waiting for transfers between devices  12.8 us (17%)
  local copies, waits for them, and re-layouts  5.82 us (8%)
  between operations  0.76 us (1%)
    ppermute x8, starting transfers between devices, shifted(): lax.ppermute(block, axis, [(i, i + step) for i in range(count) if 0 <= i...  33 us
    ppermute x8, waiting for transfers between devices, shifted(): lax.ppermute(block, axis, [(i, i + step) for i in range(count) if 0 <= i...  12.8 us
    pallas_call x1, Pallas kernels, body(): call(gather_update, [(6, 8, 8, 128), (5, 64, 128), (64, 8, 128), (16, 8,...  12.5 us
    unnamed x20, local copies, waits for them, and re-layouts  4.98 us
    pallas_call x1, Pallas kernels, body(): call(scatter, [(6, 8, 8, 128)])(stepped, sources, home_cell_index)  3.58 us
    pallas_call x1, Pallas kernels, body(): call(pack_z, [(6, 12, 16, 128), (6, 16, 128)])(gas, rows, ylo, yhi)  2.06 us
    pallas_call x1, Pallas kernels, body(): call(place, [(64, 5, 128)], in_specs=[smem, smem] + [vmem] * 3)  1.88 us
    pallas_call x1, Pallas kernels, body(): call(pack_y, [(6, 4, 8, 128), (6, 3, 8, 128), (6, 3, 8, 128)])  1.65 us
  transfers between devices with their start and end apart: 8, of which 3 were waited for; matrix products, arithmetic and copies ran while one was open for 1% of the time, Pallas kernels for 5%

profile of v1, /device:TPU:35, one launch (start us, length us, event | category | flops | bytes accessed | tf_op | source)
XLA Modules:
  0.0 74.0 jit_solution(7178006885576706863)
XLA Ops:
  0.6 0.8 %fusion = (f32[6,2,8,128]{3,2,1,0:T(8,128)S(1)}, f32[6,2,8,128]{3,2,1,0:T(8,128)S(1)}) fusion(f32[6,8,8,128]{3,2,1,0:T(8,128)} %gas.3), kind=kLoop, calls=%fused_computation | loop fusion | bytes 196608 | tf_op jit(solution)/shard_map/slice | solution.py:395
  1.5 10.6 %collective-permute-start.1 = (f32[6,2,8,128]{3,2,1,0:T(8,128)S(1)}, f32[6,2,8,128]{3,2,1,0:T(8,128)S(1)}, u32[]{:S(2)}, u32[]{:S(2)}) collective-permute-start(f32[6,2,8,128]{3,2,1,0:T(8,128)S(1)} %get-tuple-element.24), channel_id=1, source_target_pairs={{32,0},{64,32},{96,64},{128,96},{160,128},{192,160},{224,192},{256... | collective-permute-start | bytes 147464 | tf_op jit(solution)/shard_map/ppermute | solution.py:25
  12.1 1.9 %collective-permute-start = (f32[6,2,8,128]{3,2,1,0:T(8,128)S(1)}, f32[6,2,8,128]{3,2,1,0:T(8,128)S(1)}, u32[]{:S(2)}, u32[]{:S(2)}) collective-permute-start(f32[6,2,8,128]{3,2,1,0:T(8,128)S(1)} %get-tuple-element.25), channel_id=1, source_target_pairs={{0,32},{32,64},{64,96},{96,128},{128,160},{160,192},{192,224},{224... | collective-permute-start | bytes 147464 | tf_op jit(solution)/shard_map/ppermute | solution.py:25
  14.0 0.0 collective-permute-done.1.xhi
  14.0 0.0 copy-start.7
  14.1 5.1 %collective-permute-done.xlo = f32[6,2,8,128]{3,2,1,0:T(8,128)S(1)} collective-permute-done((f32[6,2,8,128]{3,2,1,0:T(8,128)S(1)}, f32[6,2,8,128]{3,2,1,0:T(8,128)S(1)}, u32[]{:S(2)}, u32[]{:S(2)}) %collective-permute-start) | collective-permute-done | bytes 49184 | tf_op jit(solution)/shard_map/ppermute | solution.py:25
  19.1 0.0 copy-done.7
  19.1 0.6 copy-done.8
  19.8 1.7 %shard_map.68 = (f32[6,4,8,128]{3,2,1,0:T(8,128)}, f32[6,3,8,128]{3,2,1,0:T(8,128)}, f32[6,3,8,128]{3,2,1,0:T(8,128)}) custom-call(f32[6,8,8,128]{3,2,1,0:T(8,128)} %gas.3, f32[6,2,8,128]{3,2,1,0:T(8,128)} %copy-done.8, f32[6,2,8,128]{3,2,1,0:T(8,128)} %copy-done.7), custom_call_target="tpu_custom_call" | custom-call | tf_op jit(solution)/shard_map/pallas_call | solution.py:396
  21.4 5.9 %collective-permute-start.2 = (f32[6,3,8,128]{3,2,1,0:T(8,128)}, f32[6,3,8,128]{3,2,1,0:T(8,128)S(1)}, u32[]{:S(2)}, u32[]{:S(2)}) collective-permute-start(f32[6,3,8,128]{3,2,1,0:T(8,128)} %get-tuple-element.13), channel_id=1, source_target_pairs={{0,8},{8,16},{16,24},{1,9},{9,17},{17,25},{2,10},{10,18},{18,26},{... | collective-permute-start | bytes 221192 | tf_op jit(solution)/shard_map/ppermute | solution.py:25
  27.4 1.9 %collective-permute-start.3 = (f32[6,3,8,128]{3,2,1,0:T(8,128)}, f32[6,3,8,128]{3,2,1,0:T(8,128)S(1)}, u32[]{:S(2)}, u32[]{:S(2)}) collective-permute-start(f32[6,3,8,128]{3,2,1,0:T(8,128)} %get-tuple-element.14), channel_id=1, source_target_pairs={{8,0},{16,8},{24,16},{9,1},{17,9},{25,17},{10,2},{18,10},{26,18},{... | collective-permute-start | bytes 221192 | tf_op jit(solution)/shard_map/ppermute | solution.py:25
  29.3 0.0 collective-permute-done.2.ylo
  29.3 0.0 copy-start.1
  29.3 5.4 %collective-permute-done.3.yhi = f32[6,3,8,128]{3,2,1,0:T(8,128)S(1)} collective-permute-done((f32[6,3,8,128]{3,2,1,0:T(8,128)}, f32[6,3,8,128]{3,2,1,0:T(8,128)S(1)}, u32[]{:S(2)}, u32[]{:S(2)}) %collective-permute-start.3) | collective-permute-done | bytes 73760 | tf_op jit(solution)/shard_map/ppermute | solution.py:25
  34.7 0.6 copy-done.2
  35.4 2.1 %shard_map.69 = (f32[6,12,16,128]{3,2,1,0:T(8,128)}, f32[6,16,128]{2,1,0:T(8,128)}) custom-call(f32[6,8,8,128]{3,2,1,0:T(8,128)} %gas.3, f32[6,4,8,128]{3,2,1,0:T(8,128)} %get-tuple-element.12.rows, f32[6,3,8,128]{3,2,1,0:T(8,128)} %copy-done.1, f32[6,3,8,128]{3,2,1,0:T(8,128)} %copy-done.2), custom_call_target="tpu_custom_call" | custom-call | tf_op jit(solution)/shard_map/pallas_call | solution.py:399
  37.4 2.1 %collective-permute-start.5 = (f32[6,16,128]{2,1,0:T(8,128)}, f32[6,16,128]{2,1,0:T(8,128)S(1)}, u32[]{:S(2)}, u32[]{:S(2)}) collective-permute-start(f32[6,16,128]{2,1,0:T(8,128)} %get-tuple-element.16.own), channel_id=1, source_target_pairs={{1,0},{2,1},{3,2},{4,3},{5,4},{6,5},{7,6},{9,8},{10,9},{11,10},{12... | collective-permute-start | bytes 147464 | tf_op jit(solution)/shard_map/ppermute | solution.py:25
  39.5 3.2 %collective-permute-start.4 = (f32[6,16,128]{2,1,0:T(8,128)}, f32[6,16,128]{2,1,0:T(8,128)S(1)}, u32[]{:S(2)}, u32[]{:S(2)}) collective-permute-start(f32[6,16,128]{2,1,0:T(8,128)} %get-tuple-element.16.own), channel_id=1, source_target_pairs={{0,1},{1,2},{2,3},{3,4},{4,5},{5,6},{6,7},{8,9},{9,10},{10,11},{11... | collective-permute-start | bytes 147464 | tf_op jit(solution)/shard_map/ppermute | solution.py:25
  42.7 0.8 %copy.7.parcels = f32[64,5,128]{2,1,0:T(8,128)} copy(f32[64,5,128]{2,0,1:T(8,128)S(1)} %copy-done) | data formatting | bytes 327680 | tf_op args[1]
  43.5 0.0 collective-permute-done.5.above
  43.5 2.2 %collective-permute-done.4.below = f32[6,16,128]{2,1,0:T(8,128)S(1)} collective-permute-done((f32[6,16,128]{2,1,0:T(8,128)}, f32[6,16,128]{2,1,0:T(8,128)S(1)}, u32[]{:S(2)}, u32[]{:S(2)}) %collective-permute-start.4) | collective-permute-done | bytes 49184 | tf_op jit(solution)/shard_map/ppermute | solution.py:25
  45.8 0.6 copy-done.6
  46.4 12.5 %shard_map.70 = (f32[6,8,8,128]{3,2,1,0:T(8,128)}, f32[5,64,128]{2,1,0:T(8,128)}, f32[64,8,128]{2,1,0:T(8,128)}, f32[16,8,128]{2,1,0:T(8,128)}, f32[16,8,128]{2,1,0:T(8,128)}) custom-call(s32[1,64]{1,0:T(1,128)} %order.3, s32[1,3]{1,0:T(1,128)} %counts.3, f32[6,12,16,128]{3,2,1,0:T(8,128)} %get-tuple-element.15.box, f32[6,16,128]{2,1,0:T(8,128)} %get-tuple-element.16.own, ...), custom_call_target="tpu_custom_call" | custom-call | tf_op jit(solution)/shard_map/pallas_call | solution.py:402
  58.8 1.9 %collective-permute-start.6 = (f32[16,8,128]{2,1,0:T(8,128)}, f32[16,8,128]{2,1,0:T(8,128)S(1)}, u32[]{:S(2)}, u32[]{:S(2)}) collective-permute-start(f32[16,8,128]{2,1,0:T(8,128)} %get-tuple-element.20), channel_id=1, source_target_pairs={{0,32},{32,64},{64,96},{96,128},{128,160},{160,192},{192,224},{224... | collective-permute-start | bytes 196616 | tf_op jit(solution)/shard_map/ppermute | solution.py:25
  60.7 5.5 %collective-permute-start.7 = (f32[16,8,128]{2,1,0:T(8,128)}, f32[16,8,128]{2,1,0:T(8,128)S(1)}, u32[]{:S(2)}, u32[]{:S(2)}) collective-permute-start(f32[16,8,128]{2,1,0:T(8,128)} %get-tuple-element.21), channel_id=1, source_target_pairs={{32,0},{64,32},{96,64},{128,96},{160,128},{192,160},{224,192},{256... | collective-permute-start | bytes 196616 | tf_op jit(solution)/shard_map/ppermute | solution.py:25
  66.2 3.6 %shard_map.71 = f32[6,8,8,128]{3,2,1,0:T(8,128)} custom-call(f32[6,8,8,128]{3,2,1,0:T(8,128)} %get-tuple-element.17.stepped, f32[5,64,128]{2,1,0:T(8,128)} %get-tuple-element.18.sources, s32[64,128]{1,0:T(8,128)} %cells.3), custom_call_target="tpu_custom_call" | custom-call | tf_op jit(solution)/shard_map/pallas_call | solution.py:415
  69.8 0.0 collective-permute-done.6.lower
  69.8 0.0 collective-permute-done.7.upper
  69.8 0.6 copy-done.3
  70.4 0.0 copy-done.4
  70.5 1.9 %shard_map.72 = f32[64,5,128]{2,1,0:T(8,128)} custom-call(s32[1,64]{1,0:T(1,128)} %order.3, s32[1,3]{1,0:T(1,128)} %counts.3, f32[64,8,128]{2,1,0:T(8,128)} %get-tuple-element.19.updated, f32[16,8,128]{2,1,0:T(8,128)} %copy-done.3, f32[16,8,128]{2,1,0:T(8,128)} %copy-done.4), custom_call_target="tpu_custom_call" | custom-call | tf_op jit(solution)/shard_map/pallas_call | solution.py:416
  72.3 1.6 %copy.8 = f32[64,5,128]{2,0,1:T(8,128)} copy(f32[64,5,128]{2,1,0:T(8,128)} %shard_map.72) | data formatting | bytes 327680
  (10 shorter events, 0.0 us)
Async XLA Ops:
  1.5 12.6 %collective-permute-start.1 = (f32[6,2,8,128]{3,2,1,0:T(8,128)S(1)}, f32[6,2,8,128]{3,2,1,0:T(8,128)S(1)}, u32[]{:S(2)}, u32[]{:S(2)}) collective-permute-start(f32[6,2,8,128]{3,2,1,0:T(8,128)S(1)} %get-tuple-element.24), channel_id=1, source_target_pairs={{32,0},{64,32},{96,64},{128,96},{160,128},{192,160},{224,192},{256... | collective-permute-start | bytes 147464 | tf_op jit(solution)/shard_map/ppermute | solution.py:25
  12.1 7.0 %collective-permute-start = (f32[6,2,8,128]{3,2,1,0:T(8,128)S(1)}, f32[6,2,8,128]{3,2,1,0:T(8,128)S(1)}, u32[]{:S(2)}, u32[]{:S(2)}) collective-permute-start(f32[6,2,8,128]{3,2,1,0:T(8,128)S(1)} %get-tuple-element.25), channel_id=1, source_target_pairs={{0,32},{32,64},{64,96},{96,128},{128,160},{160,192},{192,224},{224... | collective-permute-start | bytes 147464 | tf_op jit(solution)/shard_map/ppermute | solution.py:25
  14.0 5.1 %copy-start.7 = (f32[6,2,8,128]{3,2,1,0:T(8,128)}, f32[6,2,8,128]{3,2,1,0:T(8,128)S(1)}, u32[]{:S(2)}) copy-start(f32[6,2,8,128]{3,2,1,0:T(8,128)S(1)} %collective-permute-done.1.xhi) | copy-start | bytes 147460
  19.1 0.6 copy-start.8
  21.4 7.9 %collective-permute-start.2 = (f32[6,3,8,128]{3,2,1,0:T(8,128)}, f32[6,3,8,128]{3,2,1,0:T(8,128)S(1)}, u32[]{:S(2)}, u32[]{:S(2)}) collective-permute-start(f32[6,3,8,128]{3,2,1,0:T(8,128)} %get-tuple-element.13), channel_id=1, source_target_pairs={{0,8},{8,16},{16,24},{1,9},{9,17},{17,25},{2,10},{10,18},{18,26},{... | collective-permute-start | bytes 221192 | tf_op jit(solution)/shard_map/ppermute | solution.py:25
  27.4 7.4 %collective-permute-start.3 = (f32[6,3,8,128]{3,2,1,0:T(8,128)}, f32[6,3,8,128]{3,2,1,0:T(8,128)S(1)}, u32[]{:S(2)}, u32[]{:S(2)}) collective-permute-start(f32[6,3,8,128]{3,2,1,0:T(8,128)} %get-tuple-element.14), channel_id=1, source_target_pairs={{8,0},{16,8},{24,16},{9,1},{17,9},{25,17},{10,2},{18,10},{26,18},{... | collective-permute-start | bytes 221192 | tf_op jit(solution)/shard_map/ppermute | solution.py:25
  29.3 5.5 %copy-start.1 = (f32[6,3,8,128]{3,2,1,0:T(8,128)}, f32[6,3,8,128]{3,2,1,0:T(8,128)S(1)}, u32[]{:S(2)}) copy-start(f32[6,3,8,128]{3,2,1,0:T(8,128)S(1)} %collective-permute-done.2.ylo) | copy-start | bytes 221188
  34.7 0.6 copy-start.2
  35.4 7.3 %copy-start = (f32[64,5,128]{2,0,1:T(8,128)S(1)}, f32[64,5,128]{2,0,1:T(8,128)}, u32[]{:S(2)}) copy-start(f32[64,5,128]{2,0,1:T(8,128)} %param.6) | copy-start | bytes 491524
  37.4 6.1 %collective-permute-start.5 = (f32[6,16,128]{2,1,0:T(8,128)}, f32[6,16,128]{2,1,0:T(8,128)S(1)}, u32[]{:S(2)}, u32[]{:S(2)}) collective-permute-start(f32[6,16,128]{2,1,0:T(8,128)} %get-tuple-element.16.own), channel_id=1, source_target_pairs={{1,0},{2,1},{3,2},{4,3},{5,4},{6,5},{7,6},{9,8},{10,9},{11,10},{12... | collective-permute-start | bytes 147464 | tf_op jit(solution)/shard_map/ppermute | solution.py:25
  39.5 6.3 %collective-permute-start.4 = (f32[6,16,128]{2,1,0:T(8,128)}, f32[6,16,128]{2,1,0:T(8,128)S(1)}, u32[]{:S(2)}, u32[]{:S(2)}) collective-permute-start(f32[6,16,128]{2,1,0:T(8,128)} %get-tuple-element.16.own), channel_id=1, source_target_pairs={{0,1},{1,2},{2,3},{3,4},{4,5},{5,6},{6,7},{8,9},{9,10},{10,11},{11... | collective-permute-start | bytes 147464 | tf_op jit(solution)/shard_map/ppermute | solution.py:25
  43.5 2.2 %copy-start.5 = (f32[6,16,128]{2,1,0:T(8,128)}, f32[6,16,128]{2,1,0:T(8,128)S(1)}, u32[]{:S(2)}) copy-start(f32[6,16,128]{2,1,0:T(8,128)S(1)} %collective-permute-done.5.above) | copy-start | bytes 147460
  45.8 0.6 copy-start.6
  58.8 11.0 %collective-permute-start.6 = (f32[16,8,128]{2,1,0:T(8,128)}, f32[16,8,128]{2,1,0:T(8,128)S(1)}, u32[]{:S(2)}, u32[]{:S(2)}) collective-permute-start(f32[16,8,128]{2,1,0:T(8,128)} %get-tuple-element.20), channel_id=1, source_target_pairs={{0,32},{32,64},{64,96},{96,128},{128,160},{160,192},{192,224},{224... | collective-permute-start | bytes 196616 | tf_op jit(solution)/shard_map/ppermute | solution.py:25
  60.7 9.1 %collective-permute-start.7 = (f32[16,8,128]{2,1,0:T(8,128)}, f32[16,8,128]{2,1,0:T(8,128)S(1)}, u32[]{:S(2)}, u32[]{:S(2)}) collective-permute-start(f32[16,8,128]{2,1,0:T(8,128)} %get-tuple-element.21), channel_id=1, source_target_pairs={{32,0},{64,32},{96,64},{128,96},{160,128},{192,160},{224,192},{256... | collective-permute-start | bytes 196616 | tf_op jit(solution)/shard_map/ppermute | solution.py:25
  69.8 0.6 copy-start.3
  69.8 0.6 copy-start.4

commit v2 on v1

v2 whole, which is shorter than its diff:
```python
import jax
import jax.numpy as jnp
from jax import lax
from jax.experimental import pallas as pl
from jax.experimental.pallas import tpu as pltpu
from jax.sharding import PartitionSpec as P

GAMMA = 1.4
TIME_STEP = 0.1
RATE = 3.0
ACTIVATION = 2.0
HEAT = 5.0
DRAG_RELAX_TIME = 0.4
HEATING_RELAX = 0.6
EVAP_RATE = 1.5
LIQUID_HEAT = 2.0

F32 = jnp.float32
BF16 = jnp.bfloat16
INTERPRET = False


def shifted(block, axis, step):
    count = lax.axis_size(axis)
    return lax.ppermute(block, axis, [(i, i + step) for i in range(count) if 0 <= i + step < count])


def ends(axis):
    at = lax.axis_index(axis)
    return at == 0, at == lax.axis_size(axis) - 1


def call(kernel, outs, scalars, arrays, to=pltpu.VMEM, **kwargs):
    outs = [out if isinstance(out[0], tuple) else (out, F32) for out in outs]
    specs = [pl.BlockSpec(memory_space=pltpu.SMEM)] * len(scalars)
    specs += [pl.BlockSpec(memory_space=pltpu.VMEM)] * len(arrays)
    if not INTERPRET:
        arrays = [pltpu.with_memory_space_constraint(a, pltpu.VMEM) for a in arrays]
    make = jax.ShapeDtypeStruct if INTERPRET else to
    return pl.pallas_call(
        kernel,
        out_shape=[make(shape, dtype) for shape, dtype in outs],
        in_specs=specs,
        out_specs=[pl.BlockSpec(memory_space=pltpu.VMEM)] * len(outs),
        interpret=INTERPRET,
        **kwargs,
    )(*scalars, *arrays)


def sublane(shape):
    return lax.broadcasted_iota(jnp.int32, shape, len(shape) - 2)


def lane(shape):
    return lax.broadcasted_iota(jnp.int32, shape, len(shape) - 1)


def turn(v, shift, axis):
    size = v.shape[axis]
    shift %= size
    return v if shift == 0 else pltpu.roll(v, shift, axis)


def pack_y(gas, xlo, xhi, rows, low_pay, high_pay):
    first, last = ends("gx")
    sub = sublane((8, 128))
    for c in range(6):
        line = []
        for i in range(12):
            if i < 2:
                line.append(jnp.where(first, gas[c, 0], xlo[c, i]))
                rows[c, i] = line[-1]
            elif i < 10:
                line.append(gas[c, i - 2])
            else:
                line.append(jnp.where(last, gas[c, 7], xhi[c, i - 10]))
                rows[c, i - 8] = line[-1]
        for g in range(3):
            low = line[4 * g]
            high = turn(line[4 * g], 2, 0)
            for k in range(1, 4):
                here = (sub >= 2 * k) & (sub < 2 * k + 2)
                low = jnp.where(here, turn(line[4 * g + k], 2 * k, 0), low)
                high = jnp.where(here, turn(line[4 * g + k], 2 * k + 2, 0), high)
            low_pay[c, g] = low
            high_pay[c, g] = high


def pack_z(gas, rows, ylo, yhi, box, pay):
    first, last = ends("gy")
    sub = sublane((8, 128))
    group = lane((16, 128)) // 8
    for c in range(6):
        packed = None
        for i in range(12):
            if 2 <= i < 10:
                mid = gas[c, i - 2]
            else:
                mid = rows[c, i if i < 2 else i - 8]
            g, k = i // 4, i % 4
            below = turn(ylo[c, g], 6 - 2 * k, 0)
            above = turn(yhi[c, g], -2 * k, 0)
            below = jnp.where(first, jnp.broadcast_to(mid[0:1], (8, 128)), below)
            above = jnp.where(last, jnp.broadcast_to(mid[7:8], (8, 128)), above)
            line = jnp.concatenate([mid, jnp.where(sub < 4, above, below)], axis=0)
            box[c, i] = line
            moved = turn(line, 8 * i + 2, 1)
            packed = moved if packed is None else jnp.where(group == i, moved, packed)
        pay[c] = packed


def primitives(state):
    r, m1, m2, m3, e, _ = state
    inv = 1.0 / r
    u = (m1 * inv, m2 * inv, m3 * inv)
    p = (GAMMA - 1.0) * (e - 0.5 * (m1 * u[0] + m2 * u[1] + m3 * u[2]))
    return u, p, jnp.sqrt(GAMMA * p * inv)


def along(state, prim, k):
    u, p, sound = prim
    uk = u[k]
    flux = [state[1 + k], state[1] * uk, state[2] * uk, state[3] * uk, (state[4] + p) * uk, state[5] * uk]
    flux[1 + k] = flux[1 + k] + p
    return flux, jnp.abs(uk) + sound, state


def face(lower, upper):
    speed = jnp.maximum(lower[1], upper[1])
    return [
        (fa + fb) - speed * (b - a)
        for fa, fb, a, b in zip(lower[0], upper[0], lower[2], upper[2], strict=True)
    ]


def over(part, move):
    flux, speed, state = part
    return [move(f) for f in flux], move(speed), [move(v) for v in state]


def advanced(state, prim, total):
    burned = RATE * state[5] * jnp.exp(-ACTIVATION * state[0] / prim[1])
    out = [v - (0.5 * TIME_STEP) * t for v, t in zip(state, total, strict=True)]
    out[4] = out[4] + (TIME_STEP * HEAT) * burned
    out[5] = out[5] - TIME_STEP * burned
    return out


def cyclic_net(state, prim, k, distance, axis):
    part = along(state, prim, k)
    faces = face(part, over(part, lambda v: turn(v, -distance, axis)))
    return faces, [f - turn(f, distance, axis) for f in faces]


def side_state(own, below, above, first, last):
    at = lane((16, 128)) % 8
    low = jnp.where(at < 2, jnp.where(first, jnp.where(at == 0, turn(own, -2, 1), turn(own, -1, 1)), below), own)
    high = jnp.where(at < 2, own, jnp.where(last, jnp.where(at == 2, turn(own, 1, 1), turn(own, 2, 1)), above))
    return jnp.where(at < 4, low, turn(high, 4, 1))


def side_inflow(faces):
    at = lane((16, 128)) % 8
    return [jnp.where(at == 0, turn(f, -5, 1), -f) for f in faces]


def closed_net(part):
    faces = face(part, over(part, lambda v: turn(v, -1, 1)))
    faces = [jnp.where(lane(f.shape) == 127, 0.0, f) for f in faces]
    return [f - turn(f, 1, 1) for f in faces]


def outer(inflow, i):
    at = lane(inflow.shape)
    return jnp.where((at == 0) | (at == 127), turn(inflow, 127 - 8 * i, 1), 0.0)


def clamp_y(v):
    first, last = ends("gy")
    sub = sublane(v.shape)
    v = jnp.where(first & (sub == 15), jnp.broadcast_to(v[0:1], v.shape), v)
    return jnp.where(last & (sub == 8), jnp.broadcast_to(v[7:8], v.shape), v)


def stage_one(box, ahead):
    state = [box[c, 0] for c in range(6)]
    part = along(state, primitives(state), 0)
    state = [box[c, 1] for c in range(6)]
    prim = primitives(state)
    next_part = along(state, prim, 0)
    faces = face(part, next_part)
    for i in range(1, 11):
        part = next_part
        next_state = [box[c, i + 1] for c in range(6)]
        next_prim = primitives(next_state)
        next_part = along(next_state, next_prim, 0)
        next_faces = face(part, next_part)
        _, net_y = cyclic_net(state, prim, 1, 1, 0)
        net_z = closed_net(along(state, prim, 2))
        total = [b - a + y + z for a, b, y, z in zip(faces, next_faces, net_y, net_z, strict=True)]
        for c, v in enumerate(advanced(state, prim, total)):
            ahead[c, i] = v
        state, prim, faces = next_state, next_prim, next_faces


def sides(own, below, above):
    first_x, last_x = ends("gx")
    first_z, last_z = ends("gz")
    at = lane((16, 128)) % 8
    group = lane((16, 128)) // 8

    def clamp_x_z(v):
        v = jnp.where(first_x & (group == 1), turn(v, -8, 1), v)
        v = jnp.where(last_x & (group == 10), turn(v, 8, 1), v)
        v = jnp.where(first_z & (at == 1), turn(v, -1, 1), v)
        return jnp.where(last_z & (at == 6), turn(v, 1, 1), v)

    side = [side_state(own[c], below[c], above[c], first_z, last_z) for c in range(6)]
    prim = primitives(side)
    faces, net_z = cyclic_net(side, prim, 2, 1, 1)
    one = side_inflow(faces)
    _, net_x = cyclic_net(side, prim, 0, 8, 1)
    _, net_y = cyclic_net(side, prim, 1, 1, 0)
    side = advanced(side, prim, [x + y + z for x, y, z in zip(net_x, net_y, net_z, strict=True)])
    side = [clamp_y(clamp_x_z(v)) for v in side]
    return one, side_inflow(cyclic_net(side, primitives(side), 2, 1, 1)[0])


def stage_two(box, ahead, one, two, stepped, fields):
    first_x, last_x = ends("gx")

    def line(i):
        out = []
        for c in range(6):
            out.append(clamp_y(ahead[c, i] - (0.5 * TIME_STEP) * outer(one[c], i)))
        return out

    def row(i):
        v = line(i)
        if i == 1:
            v = [jnp.where(first_x, b, a) for a, b in zip(v, line(2), strict=True)]
        if i == 10:
            v = [jnp.where(last_x, b, a) for a, b in zip(v, line(9), strict=True)]
        return v

    def inner(values):
        return [v[:8] for v in values]

    def inner_prim(prim):
        return inner(prim[0]), prim[1][:8], prim[2][:8]

    state = inner(row(1))
    part = along(state, primitives(state), 0)
    full = row(2)
    full_prim = primitives(full)
    state, prim = inner(full), inner_prim(full_prim)
    next_part = along(state, prim, 0)
    faces = face(part, next_part)
    for i in range(2, 10):
        part = next_part
        next_full = row(i + 1)
        next_full_prim = primitives(next_full)
        next_state, next_prim = inner(next_full), inner_prim(next_full_prim)
        next_part = along(next_state, next_prim, 0)
        next_faces = face(part, next_part)
        _, net_y = cyclic_net(full, full_prim, 1, 1, 0)
        net_z = closed_net(along(state, prim, 2))
        total = [
            b - a + y[:8] + z + outer(s[:8], i)
            for a, b, y, z, s in zip(faces, next_faces, net_y, net_z, two, strict=True)
        ]
        x = i - 2
        done = [0.5 * box[c, i, 0:8] + 0.5 * v for c, v in enumerate(advanced(state, prim, total))]
        for c in range(6):
            stepped[c, x] = done[c]
        inv = 1.0 / done[0]
        g = [done[1 + k] * inv for k in range(3)]
        t = (GAMMA - 1.0) * (done[4] - 0.5 * (done[1] * g[0] + done[2] * g[1] + done[3] * g[2])) * inv
        for f, v in enumerate((*g, t, done[5] * inv)):
            fields[f, pl.ds(8 * (x % 4), 8), pl.ds(128 * (x // 4), 128)] = v
        full, full_prim, state, prim, faces = next_full, next_full_prim, next_state, next_prim, next_faces


def two_parts(v):
    big = v.astype(BF16)
    return big, (v - big.astype(F32)).astype(BF16)


def split_cell(cells):
    return (cells >> 7) & 31, ((cells >> 12) << 7) | (cells & 127)


def one_hot(index, count):
    return jnp.where(sublane((count, index.shape[-1])) == index, 1.0, 0.0).astype(BF16)


def in_order(order, parcels, cells, sorted_parcels, sorted_cells):
    for j in range(64):
        b = order[0, j]
        sorted_cells[j : j + 1, :] = cells[pl.ds(b, 1), :]
        for k in range(5):
            sorted_parcels[k, j : j + 1, :] = parcels[k, pl.ds(b, 1), :]


def alive(counts):
    return counts[0, 0] + counts[0, 1] + counts[0, 2]


def gather_update(counts, box, ahead, own, below, above, parcels, cells, stepped, sources, updated, front, back, fields, table, carried):
    one, two = sides(own, below, above)
    stage_two(box, ahead, one, two, stepped, fields)
    for f in range(5):
        big, small = two_parts(fields[f])
        table[pl.ds(32 * f, 32), :] = big
        table[pl.ds(160 + 32 * f, 32), :] = small

    total = alive(counts)

    def chunk(n, _):
        start = pl.multiple_of(8 * n, 8)
        index = cells[pl.ds(start, 8), :]
        values = [[] for _ in range(5)]
        for b in range(0, 8, 2):
            pair = jnp.concatenate([index[b : b + 1], index[b + 1 : b + 2]], axis=1)
            row, column = split_cell(pair)
            found = jnp.dot(table[...], one_hot(column, 256), preferred_element_type=F32)
            chosen = sublane((32, 256)) == row
            for f in range(5):
                both = found[32 * f : 32 * f + 32] + found[160 + 32 * f : 192 + 32 * f]
                value = jnp.sum(jnp.where(chosen, both, 0.0), axis=0, keepdims=True)
                values[f] += [value[:, :128], value[:, 128:]]
        for f in range(5):
            carried[f, pl.ds(start, 8), :] = jnp.concatenate(values[f], axis=0)
        return 0

    lax.fori_loop(0, (total + 7) // 8, chunk, 0)

    g = tuple(carried[k] for k in range(3))
    t, y = carried[3], carried[4]
    v = tuple(parcels[k] for k in range(3))
    mass, heat = parcels[3], parcels[4]
    root = jnp.sqrt(mass)
    inv_root = 1.0 / root
    new_mass = mass * jnp.exp((-TIME_STEP * EVAP_RATE) * t / (root * (1.0 + y * y)))
    slow = jnp.exp((-TIME_STEP / DRAG_RELAX_TIME) * inv_root)
    new_v = tuple(gk + (vk - gk) * slow for gk, vk in zip(g, v, strict=True))
    new_heat = t + (heat - t) * jnp.exp((-TIME_STEP / HEATING_RELAX) * inv_root)
    live = sublane((64, 128)) < total
    square = v[0] * v[0] + v[1] * v[1] + v[2] * v[2]
    new_square = new_v[0] * new_v[0] + new_v[1] * new_v[1] + new_v[2] * new_v[2]
    gain = [mass - new_mass]
    gain += [mass * v[k] - new_mass * new_v[k] for k in range(3)]
    gain += [0.5 * (mass * square - new_mass * new_square) + LIQUID_HEAT * (mass * heat - new_mass * new_heat)]
    for k in range(5):
        sources[k] = jnp.where(live, gain[k], 0.0)
    for k, value in enumerate((*new_v, new_mass, new_heat)):
        updated[k] = value

    kept, forward, backward = counts[0, 0], counts[0, 1], counts[0, 2]
    for out, start, size in ((front, kept, forward), (back, kept + forward, backward)):
        for k in range(5):
            out[k] = updated[k, pl.ds(start, 16), :]
        out[5] = jnp.full((16, 128), size.astype(F32))


def scatter(counts, stepped, sources, cells, gas_out, total):
    total[...] = jnp.zeros(total.shape, F32)

    def chunk(n, _):
        start = pl.multiple_of(8 * n, 8)
        index = cells[pl.ds(start, 8), :]
        given = [two_parts(sources[k, pl.ds(start, 8), :]) for k in range(5)]
        given = [[part.astype(F32) for part in parts] for parts in given]
        columns, wide = [], []
        for b in range(8):
            row, column = split_cell(index[b : b + 1, :])
            columns.append(one_hot(column, 256))
            chosen = sublane((32, 128)) == row
            wide.append(
                jnp.concatenate(
                    [
                        jnp.where(chosen, jnp.broadcast_to(given[k][half][b : b + 1, :], (32, 128)), 0.0).astype(BF16)
                        for half in range(2)
                        for k in range(5)
                    ],
                    axis=0,
                )
            )
        total[...] += lax.dot_general(
            jnp.concatenate(wide, axis=1),
            jnp.concatenate(columns, axis=1),
            (((1,), (1,)), ((), ())),
            preferred_element_type=F32,
        )
        return 0

    lax.fori_loop(0, (alive(counts) + 7) // 8, chunk, 0)
    for c in range(6):
        k = c % 5
        both = total[32 * k : 32 * k + 32] + total[160 + 32 * k : 192 + 32 * k]
        for half in range(2):
            added = jnp.reshape(both[:, 128 * half : 128 * half + 128], (4, 8, 128))
            gas_out[c, 4 * half : 4 * half + 4] = stepped[c, 4 * half : 4 * half + 4] + added


def place(counts, updated, lower, upper, moved):
    kept = counts[0, 0]
    first, last = ends("gx")
    from_lower = jnp.where(first, 0.0, lower[5, 0, 0]).astype(jnp.int32)
    from_upper = jnp.where(last, 0.0, upper[5, 0, 0]).astype(jnp.int32)
    slot = sublane((64, 128))
    near = sublane((16, 128))
    for k in range(5):
        moved[k] = jnp.where(slot < kept, updated[k], 0.0)
    for k in range(5):
        moved[k, pl.ds(kept, 16), :] = jnp.where(near < from_lower, lower[k], 0.0)
    for k in range(5):
        moved[k, pl.ds(kept + from_lower, 16), :] = jnp.where(near < from_upper, upper[k], 0.0)


def body(gas, parcels, home_cell_index, order, counts):
    xlo = shifted(gas[:, 6:8], "gx", 1)
    xhi = shifted(gas[:, 0:2], "gx", -1)
    sorted_parcels, cells = call(
        in_order, [(5, 64, 128), ((64, 128), jnp.int32)], [order], [jnp.transpose(parcels, (1, 0, 2)), home_cell_index]
    )
    rows, low, high = call(pack_y, [(6, 4, 8, 128), (6, 3, 8, 128), (6, 3, 8, 128)], [], [gas, xlo, xhi])
    ylo = shifted(high, "gy", 1)
    yhi = shifted(low, "gy", -1)
    box, pay = call(pack_z, [(6, 12, 16, 128), (6, 16, 128)], [], [gas, rows, ylo, yhi])
    below = shifted(pay, "gz", 1)
    above = shifted(pay, "gz", -1)
    (ahead,) = call(stage_one, [(6, 12, 16, 128)], [], [box])
    stepped, sources, updated, front, back = call(
        gather_update,
        [(6, 8, 8, 128), (5, 64, 128), (5, 64, 128), (6, 16, 128), (6, 16, 128)],
        [counts],
        [box, ahead, pay, below, above, sorted_parcels, cells],
        scratch_shapes=[
            pltpu.VMEM((5, 32, 256), F32),
            pltpu.VMEM((320, 256), BF16),
            pltpu.VMEM((5, 64, 128), F32),
        ],
    )
    lower = shifted(front, "gx", 1)
    upper = shifted(back, "gx", -1)
    (gas_out,) = call(
        scatter,
        [(6, 8, 8, 128)],
        [counts],
        [stepped, sources, cells],
        to=pltpu.HBM,
        scratch_shapes=[pltpu.VMEM((320, 256), F32)],
    )
    (moved,) = call(place, [(5, 64, 128)], [counts], [updated, lower, upper], to=pltpu.HBM)
    return gas_out, jnp.transpose(moved, (1, 0, 2))


def solution(mesh):
    blocks = ("gx", "gy", "gz")
    in_specs = (
        P(None, *blocks),
        P(blocks, None, None),
        P(blocks, None),
        P(blocks, None),
        P(blocks, None),
    )
    out_specs = (P(None, *blocks), P(blocks, None, None))
    return jax.shard_map(body, mesh=mesh, in_specs=in_specs, out_specs=out_specs, check_vma=False)
```

time: 74.5 us -> 57.2 us (0.77)
  the two profiles are of different devices: /device:TPU:35 before, /device:TPU:27 now
where the time goes in v2:
time: 57.2 us; the launch traced here: 56.9 us
  starting transfers between devices  34.4 us (60%)
  Pallas kernels  10.5 us (18%)
  waiting for transfers between devices  10.3 us (18%)
  local copies, waits for them, and re-layouts  0.89 us (2%)
  between operations  0.78 us (1%)
    ppermute x8, starting transfers between devices, shifted(): lax.ppermute(block, axis, [(i, i + step) for i in range(count) if 0 <= i...  34.4 us
    pallas_call x7, Pallas kernels, call(): pl.pallas_call(kernel, out_shape=[make(shape, dtype) for shape, dtype in...  10.5 us
    ppermute x8, waiting for transfers between devices, shifted(): lax.ppermute(block, axis, [(i, i + step) for i in range(count) if 0 <= i...  10.3 us
  transfers between devices with their start and end apart: 8, of which 2 were waited for; matrix products, arithmetic and copies ran while one was open for 0% of the time, Pallas kernels for 9%

profile of v2, /device:TPU:27, one launch (start us, length us, event | category | flops | bytes accessed | tf_op | source)
XLA Modules:
  0.0 56.9 jit_solution(2330197408922814347)
XLA Ops:
  0.6 0.0 copy-start
  0.6 0.9 %fusion = (f32[6,2,8,128]{3,2,1,0:T(8,128)S(1)}, f32[6,2,8,128]{3,2,1,0:T(8,128)S(1)}) fusion(f32[6,8,8,128]{3,2,1,0:T(8,128)} %gas.3), kind=kLoop, calls=%fused_computation | loop fusion | bytes 196608 | tf_op jit(solution)/shard_map/slice | solution.py:423
  1.5 10.6 %collective-permute-start.1 = (f32[6,2,8,128]{3,2,1,0:T(8,128)S(1)}, f32[6,2,8,128]{3,2,1,0:T(8,128)S(1)}, u32[]{:S(2)}, u32[]{:S(2)}) collective-permute-start(f32[6,2,8,128]{3,2,1,0:T(8,128)S(1)} %get-tuple-element.26), channel_id=1, source_target_pairs={{32,0},{64,32},{96,64},{128,96},{160,128},{192,160},{224,192},{256... | collective-permute-start | bytes 147464 | tf_op jit(solution)/shard_map/ppermute | solution.py:25
  12.2 1.9 %collective-permute-start = (f32[6,2,8,128]{3,2,1,0:T(8,128)S(1)}, f32[6,2,8,128]{3,2,1,0:T(8,128)S(1)}, u32[]{:S(2)}, u32[]{:S(2)}) collective-permute-start(f32[6,2,8,128]{3,2,1,0:T(8,128)S(1)} %get-tuple-element.27), channel_id=1, source_target_pairs={{0,32},{32,64},{64,96},{96,128},{128,160},{160,192},{192,224},{224... | collective-permute-start | bytes 147464 | tf_op jit(solution)/shard_map/ppermute | solution.py:25
  14.1 0.0 collective-permute-done.1.xhi
  14.1 5.0 %collective-permute-done.xlo = f32[6,2,8,128]{3,2,1,0:T(8,128)S(1)} collective-permute-done((f32[6,2,8,128]{3,2,1,0:T(8,128)S(1)}, f32[6,2,8,128]{3,2,1,0:T(8,128)S(1)}, u32[]{:S(2)}, u32[]{:S(2)}) %collective-permute-start) | collective-permute-done | bytes 49184 | tf_op jit(solution)/shard_map/ppermute | solution.py:25
  19.1 0.0 copy-done
  19.1 6.0 %collective-permute-start.2 = (f32[6,3,8,128]{3,2,1,0:T(8,128)S(1)}, f32[6,3,8,128]{3,2,1,0:T(8,128)S(1)}, u32[]{:S(2)}, u32[]{:S(2)}) collective-permute-start(f32[6,3,8,128]{3,2,1,0:T(8,128)S(1)} %get-tuple-element.15), channel_id=1, source_target_pairs={{0,8},{8,16},{16,24},{1,9},{9,17},{17,25},{2,10},{10,18},{18,26},{... | collective-permute-start | bytes 221192 | tf_op jit(solution)/shard_map/ppermute | solution.py:25
  25.2 1.9 %collective-permute-start.3 = (f32[6,3,8,128]{3,2,1,0:T(8,128)S(1)}, f32[6,3,8,128]{3,2,1,0:T(8,128)S(1)}, u32[]{:S(2)}, u32[]{:S(2)}) collective-permute-start(f32[6,3,8,128]{3,2,1,0:T(8,128)S(1)} %get-tuple-element.16), channel_id=1, source_target_pairs={{8,0},{16,8},{24,16},{9,1},{17,9},{25,17},{10,2},{18,10},{26,18},{... | collective-permute-start | bytes 221192 | tf_op jit(solution)/shard_map/ppermute | solution.py:25
  27.1 0.0 collective-permute-done.2.ylo
  27.1 5.2 %collective-permute-done.3.yhi = f32[6,3,8,128]{3,2,1,0:T(8,128)S(1)} collective-permute-done((f32[6,3,8,128]{3,2,1,0:T(8,128)S(1)}, f32[6,3,8,128]{3,2,1,0:T(8,128)S(1)}, u32[]{:S(2)}, u32[]{:S(2)}) %collective-permute-start.3) | collective-permute-done | bytes 73760 | tf_op jit(solution)/shard_map/ppermute | solution.py:25
  32.4 0.0 copy-start.1
  32.4 0.0 copy-start.2
  32.4 0.2 shard_map.69
  32.6 2.1 %collective-permute-start.5 = (f32[6,16,128]{2,1,0:T(8,128)S(1)}, f32[6,16,128]{2,1,0:T(8,128)S(1)}, u32[]{:S(2)}, u32[]{:S(2)}) collective-permute-start(f32[6,16,128]{2,1,0:T(8,128)S(1)} %get-tuple-element.18.own), channel_id=1, source_target_pairs={{1,0},{2,1},{3,2},{4,3},{5,4},{6,5},{7,6},{9,8},{10,9},{11,10},{12... | collective-permute-start | bytes 147464 | tf_op jit(solution)/shard_map/ppermute | solution.py:25
  34.7 4.4 %collective-permute-start.4 = (f32[6,16,128]{2,1,0:T(8,128)S(1)}, f32[6,16,128]{2,1,0:T(8,128)S(1)}, u32[]{:S(2)}, u32[]{:S(2)}) collective-permute-start(f32[6,16,128]{2,1,0:T(8,128)S(1)} %get-tuple-element.18.own), channel_id=1, source_target_pairs={{0,1},{1,2},{2,3},{3,4},{4,5},{5,6},{6,7},{8,9},{9,10},{10,11},{11... | collective-permute-start | bytes 147464 | tf_op jit(solution)/shard_map/ppermute | solution.py:25
  39.1 0.0 copy-done.1
  39.1 0.0 copy-done.2
  39.1 0.9 %shard_map.71 = (f32[5,64,128]{2,1,0:T(8,128)S(1)}, s32[64,128]{1,0:T(8,128)S(1)}) custom-call(s32[1,64]{1,0:T(1,128)} %order.1, f32[5,64,128]{2,1,0:T(8,128)S(1)} %bitcast.2, s32[64,128]{1,0:T(8,128)S(1)} %copy-done.2), custom_call_target="tpu_custom_call" | custom-call | tf_op jit(solution)/shard_map/pallas_call | solution.py:40
  40.0 0.9 %shard_map.70.ahead = f32[6,12,16,128]{3,2,1,0:T(8,128)S(1)} custom-call(f32[6,12,16,128]{3,2,1,0:T(8,128)S(1)} %get-tuple-element.17.box), custom_call_target="tpu_custom_call" | custom-call | tf_op jit(solution)/shard_map/pallas_call | solution.py:40
  40.9 0.0 collective-permute-done.5.above
  40.9 0.0 collective-permute-done.4.below
  40.9 3.8 %shard_map.72 = (f32[6,8,8,128]{3,2,1,0:T(8,128)S(1)}, f32[5,64,128]{2,1,0:T(8,128)S(1)}, f32[5,64,128]{2,1,0:T(8,128)S(1)}, f32[6,16,128]{2,1,0:T(8,128)S(1)}, f32[6,16,128]{2,1,0:T(8,128)S(1)}) custom-call(s32[1,3]{1,0:T(1,128)} %counts.5, f32[6,12,16,128]{3,2,1,0:T(8,128)S(1)} %get-tuple-element.17.box, f32[6,12,16,128]{3,2,1,0:T(8,128)S(1)} %shard_map.70.ahead, ...), custom_call_target="tpu_custom_call" | custom-call | tf_op jit(solution)/shard_map/pallas_call | solution.py:40
  44.7 1.9 %collective-permute-start.6 = (f32[6,16,128]{2,1,0:T(8,128)S(1)}, f32[6,16,128]{2,1,0:T(8,128)S(1)}, u32[]{:S(2)}, u32[]{:S(2)}) collective-permute-start(f32[6,16,128]{2,1,0:T(8,128)S(1)} %get-tuple-element.24), channel_id=1, source_target_pairs={{0,32},{32,64},{64,96},{96,128},{128,160},{160,192},{192,224},{224... | collective-permute-start | bytes 147464 | tf_op jit(solution)/shard_map/ppermute | solution.py:25
  46.7 5.5 %collective-permute-start.7 = (f32[6,16,128]{2,1,0:T(8,128)S(1)}, f32[6,16,128]{2,1,0:T(8,128)S(1)}, u32[]{:S(2)}, u32[]{:S(2)}) collective-permute-start(f32[6,16,128]{2,1,0:T(8,128)S(1)} %get-tuple-element.25), channel_id=1, source_target_pairs={{32,0},{64,32},{96,64},{128,96},{160,128},{192,160},{224,192},{256... | collective-permute-start | bytes 147464 | tf_op jit(solution)/shard_map/ppermute | solution.py:25
  52.2 3.3 %shard_map.73 = f32[6,8,8,128]{3,2,1,0:T(8,128)} custom-call(s32[1,3]{1,0:T(1,128)} %counts.5, f32[6,8,8,128]{3,2,1,0:T(8,128)S(1)} %get-tuple-element.21.stepped, f32[5,64,128]{2,1,0:T(8,128)S(1)} %get-tuple-element.22.sources, s32[64,128]{1,0:T(8,128)S(1)} %get-tuple-element.20.cells), custom_call_target="tpu_custom_call" | custom-call | tf_op jit(solution)/shard_map/pallas_call | solution.py:40
  55.5 0.0 collective-permute-done.6.lower
  55.5 0.0 collective-permute-done.7.upper
  55.5 1.4 %shard_map.74 = f32[5,64,128]{2,1,0:T(8,128)} custom-call(s32[1,3]{1,0:T(1,128)} %counts.5, f32[5,64,128]{2,1,0:T(8,128)S(1)} %get-tuple-element.23.updated, f32[6,16,128]{2,1,0:T(8,128)S(1)} %collective-permute-done.6.lower, f32[6,16,128]{2,1,0:T(8,128)S(1)} %collective-permute-done.7.upper), custom_call_target="tpu_custom_call" | custom-call | tf_op jit(solution)/shard_map/pallas_call | solution.py:40
  (1 shorter events, 0.0 us)
Async XLA Ops:
  0.6 18.5 %copy-start = (f32[6,8,8,128]{3,2,1,0:T(8,128)S(1)}, f32[6,8,8,128]{3,2,1,0:T(8,128)}, u32[]{:S(2)}) copy-start(f32[6,8,8,128]{3,2,1,0:T(8,128)} %gas.3) | copy-start | bytes 589828
  1.5 12.6 %collective-permute-start.1 = (f32[6,2,8,128]{3,2,1,0:T(8,128)S(1)}, f32[6,2,8,128]{3,2,1,0:T(8,128)S(1)}, u32[]{:S(2)}, u32[]{:S(2)}) collective-permute-start(f32[6,2,8,128]{3,2,1,0:T(8,128)S(1)} %get-tuple-element.26), channel_id=1, source_target_pairs={{32,0},{64,32},{96,64},{128,96},{160,128},{192,160},{224,192},{256... | collective-permute-start | bytes 147464 | tf_op jit(solution)/shard_map/ppermute | solution.py:25
  12.2 6.9 %collective-permute-start = (f32[6,2,8,128]{3,2,1,0:T(8,128)S(1)}, f32[6,2,8,128]{3,2,1,0:T(8,128)S(1)}, u32[]{:S(2)}, u32[]{:S(2)}) collective-permute-start(f32[6,2,8,128]{3,2,1,0:T(8,128)S(1)} %get-tuple-element.27), channel_id=1, source_target_pairs={{0,32},{32,64},{64,96},{96,128},{128,160},{160,192},{192,224},{224... | collective-permute-start | bytes 147464 | tf_op jit(solution)/shard_map/ppermute | solution.py:25
  19.1 8.0 %collective-permute-start.2 = (f32[6,3,8,128]{3,2,1,0:T(8,128)S(1)}, f32[6,3,8,128]{3,2,1,0:T(8,128)S(1)}, u32[]{:S(2)}, u32[]{:S(2)}) collective-permute-start(f32[6,3,8,128]{3,2,1,0:T(8,128)S(1)} %get-tuple-element.15), channel_id=1, source_target_pairs={{0,8},{8,16},{16,24},{1,9},{9,17},{17,25},{2,10},{10,18},{18,26},{... | collective-permute-start | bytes 221192 | tf_op jit(solution)/shard_map/ppermute | solution.py:25
  25.2 7.2 %collective-permute-start.3 = (f32[6,3,8,128]{3,2,1,0:T(8,128)S(1)}, f32[6,3,8,128]{3,2,1,0:T(8,128)S(1)}, u32[]{:S(2)}, u32[]{:S(2)}) collective-permute-start(f32[6,3,8,128]{3,2,1,0:T(8,128)S(1)} %get-tuple-element.16), channel_id=1, source_target_pairs={{8,0},{16,8},{24,16},{9,1},{17,9},{25,17},{10,2},{18,10},{26,18},{... | collective-permute-start | bytes 221192 | tf_op jit(solution)/shard_map/ppermute | solution.py:25
  32.4 6.8 %copy-start.1 = (f32[64,5,128]{2,0,1:T(8,128)S(1)}, f32[64,5,128]{2,0,1:T(8,128)}, u32[]{:S(2)}) copy-start(f32[64,5,128]{2,0,1:T(8,128)} %param.6) | copy-start | bytes 491524
  32.4 6.8 %copy-start.2 = (s32[64,128]{1,0:T(8,128)S(1)}, s32[64,128]{1,0:T(8,128)}, u32[]{:S(2)}) copy-start(s32[64,128]{1,0:T(8,128)} %cells.1) | copy-start | bytes 98308
  32.6 8.3 %collective-permute-start.5 = (f32[6,16,128]{2,1,0:T(8,128)S(1)}, f32[6,16,128]{2,1,0:T(8,128)S(1)}, u32[]{:S(2)}, u32[]{:S(2)}) collective-permute-start(f32[6,16,128]{2,1,0:T(8,128)S(1)} %get-tuple-element.18.own), channel_id=1, source_target_pairs={{1,0},{2,1},{3,2},{4,3},{5,4},{6,5},{7,6},{9,8},{10,9},{11,10},{12... | collective-permute-start | bytes 147464 | tf_op jit(solution)/shard_map/ppermute | solution.py:25
  34.7 6.2 %collective-permute-start.4 = (f32[6,16,128]{2,1,0:T(8,128)S(1)}, f32[6,16,128]{2,1,0:T(8,128)S(1)}, u32[]{:S(2)}, u32[]{:S(2)}) collective-permute-start(f32[6,16,128]{2,1,0:T(8,128)S(1)} %get-tuple-element.18.own), channel_id=1, source_target_pairs={{0,1},{1,2},{2,3},{3,4},{4,5},{5,6},{6,7},{8,9},{9,10},{10,11},{11... | collective-permute-start | bytes 147464 | tf_op jit(solution)/shard_map/ppermute | solution.py:25
  44.7 10.7 %collective-permute-start.6 = (f32[6,16,128]{2,1,0:T(8,128)S(1)}, f32[6,16,128]{2,1,0:T(8,128)S(1)}, u32[]{:S(2)}, u32[]{:S(2)}) collective-permute-start(f32[6,16,128]{2,1,0:T(8,128)S(1)} %get-tuple-element.24), channel_id=1, source_target_pairs={{0,32},{32,64},{64,96},{96,128},{128,160},{160,192},{192,224},{224... | collective-permute-start | bytes 147464 | tf_op jit(solution)/shard_map/ppermute | solution.py:25
  46.7 8.8 %collective-permute-start.7 = (f32[6,16,128]{2,1,0:T(8,128)S(1)}, f32[6,16,128]{2,1,0:T(8,128)S(1)}, u32[]{:S(2)}, u32[]{:S(2)}) collective-permute-start(f32[6,16,128]{2,1,0:T(8,128)S(1)} %get-tuple-element.25), channel_id=1, source_target_pairs={{32,0},{64,32},{96,64},{128,96},{160,128},{192,160},{224,192},{256... | collective-permute-start | bytes 147464 | tf_op jit(solution)/shard_map/ppermute | solution.py:25

commit v3 on v2

--- a/solution.py
+++ b/solution.py
@@ -4,6 +4,7 @@
 from jax.experimental import pallas as pl
 from jax.experimental.pallas import tpu as pltpu
 from jax.sharding import PartitionSpec as P
+
 
 GAMMA = 1.4
 TIME_STEP = 0.1
@@ -20,9 +21,17 @@
 INTERPRET = False
 
 
-def shifted(block, axis, step):
+def swapped(blocks, axis):
     count = lax.axis_size(axis)
-    return lax.ppermute(block, axis, [(i, i + step) for i in range(count) if 0 <= i + step < count])
+    out = []
+    for first, block in enumerate(blocks):
+        pairs = [(i, i + 1) for i in range(first, count - 1, 2)]
+        out.append(lax.ppermute(block, axis, pairs + [(j, i) for i, j in pairs]))
+    return out
+
+
+def is_even(axis):
+    return lax.axis_index(axis) % 2 == 0
 
 
 def ends(axis):
@@ -30,16 +39,16 @@
     return at == 0, at == lax.axis_size(axis) - 1
 
 
-def call(kernel, outs, scalars, arrays, to=pltpu.VMEM, **kwargs):
+def call(kernel, outs, scalars, arrays, to=None, **kwargs):
     outs = [out if isinstance(out[0], tuple) else (out, F32) for out in outs]
     specs = [pl.BlockSpec(memory_space=pltpu.SMEM)] * len(scalars)
     specs += [pl.BlockSpec(memory_space=pltpu.VMEM)] * len(arrays)
     if not INTERPRET:
         arrays = [pltpu.with_memory_space_constraint(a, pltpu.VMEM) for a in arrays]
-    make = jax.ShapeDtypeStruct if INTERPRET else to
+    to = [jax.ShapeDtypeStruct if INTERPRET else space for space in to or [pltpu.VMEM] * len(outs)]
     return pl.pallas_call(
         kernel,
-        out_shape=[make(shape, dtype) for shape, dtype in outs],
+        out_shape=[space(*out) for space, out in zip(to, outs, strict=True)],
         in_specs=specs,
         out_specs=[pl.BlockSpec(memory_space=pltpu.VMEM)] * len(outs),
         interpret=INTERPRET,
@@ -61,19 +70,22 @@
     return v if shift == 0 else pltpu.roll(v, shift, axis)
 
 
-def pack_y(gas, xlo, xhi, rows, low_pay, high_pay):
+def pack_y(gas, even_pairs, odd_pairs, _, rows, even_pay, odd_pay):
     first, last = ends("gx")
+    even_x, even_y = is_even("gx"), is_even("gy")
     sub = sublane((8, 128))
     for c in range(6):
         line = []
         for i in range(12):
             if i < 2:
-                line.append(jnp.where(first, gas[c, 0], xlo[c, i]))
+                below = jnp.where(even_x, odd_pairs[c, i], even_pairs[c, i])
+                line.append(jnp.where(first, gas[c, 0], below))
                 rows[c, i] = line[-1]
             elif i < 10:
                 line.append(gas[c, i - 2])
             else:
-                line.append(jnp.where(last, gas[c, 7], xhi[c, i - 10]))
+                above = jnp.where(even_x, even_pairs[c, i - 10], odd_pairs[c, i - 10])
+                line.append(jnp.where(last, gas[c, 7], above))
                 rows[c, i - 8] = line[-1]
         for g in range(3):
             low = line[4 * g]
@@ -82,15 +94,18 @@
                 here = (sub >= 2 * k) & (sub < 2 * k + 2)
                 low = jnp.where(here, turn(line[4 * g + k], 2 * k, 0), low)
                 high = jnp.where(here, turn(line[4 * g + k], 2 * k + 2, 0), high)
-            low_pay[c, g] = low
-            high_pay[c, g] = high
-
-
-def pack_z(gas, rows, ylo, yhi, box, pay):
+            even_pay[c, g] = jnp.where(even_y, high, low)
+            odd_pay[c, g] = jnp.where(even_y, low, high)
+
+
+def pack_z(gas, rows, even_pairs, odd_pairs, box, pay):
+    even = is_even("gy")
     first, last = ends("gy")
     sub = sublane((8, 128))
     group = lane((16, 128)) // 8
     for c in range(6):
+        ylo = [jnp.where(even, odd_pairs[c, g], even_pairs[c, g]) for g in range(3)]
+        yhi = [jnp.where(even, even_pairs[c, g], odd_pairs[c, g]) for g in range(3)]
         packed = None
         for i in range(12):
             if 2 <= i < 10:
@@ -98,8 +113,8 @@
             else:
                 mid = rows[c, i if i < 2 else i - 8]
             g, k = i // 4, i % 4
-            below = turn(ylo[c, g], 6 - 2 * k, 0)
-            above = turn(yhi[c, g], -2 * k, 0)
+            below = turn(ylo[g], 6 - 2 * k, 0)
+            above = turn(yhi[g], -2 * k, 0)
             below = jnp.where(first, jnp.broadcast_to(mid[0:1], (8, 128)), below)
             above = jnp.where(last, jnp.broadcast_to(mid[7:8], (8, 128)), above)
             line = jnp.concatenate([mid, jnp.where(sub < 4, above, below)], axis=0)
@@ -203,7 +218,7 @@
         state, prim, faces = next_state, next_prim, next_faces
 
 
-def sides(own, below, above):
+def sides(own, even_pairs, odd_pairs):
     first_x, last_x = ends("gx")
     first_z, last_z = ends("gz")
     at = lane((16, 128)) % 8
@@ -215,7 +230,12 @@
         v = jnp.where(first_z & (at == 1), turn(v, -1, 1), v)
         return jnp.where(last_z & (at == 6), turn(v, 1, 1), v)
 
-    side = [side_state(own[c], below[c], above[c], first_z, last_z) for c in range(6)]
+    even = is_even("gz")
+    side = []
+    for c in range(6):
+        below = jnp.where(even, odd_pairs[c], even_pairs[c])
+        above = jnp.where(even, even_pairs[c], odd_pairs[c])
+        side.append(side_state(own[c], below, above, first_z, last_z))
     prim = primitives(side)
     faces, net_z = cyclic_net(side, prim, 2, 1, 1)
     one = side_inflow(faces)
@@ -294,28 +314,24 @@
     return jnp.where(sublane((count, index.shape[-1])) == index, 1.0, 0.0).astype(BF16)
 
 
-def in_order(order, parcels, cells, sorted_parcels, sorted_cells):
+def moving(counts):
+    return counts[0, 1] + counts[0, 2]
+
+
+def alive(counts):
+    return counts[0, 0] + moving(counts)
+
+
+def in_order(order, counts, parcels, cells, sorted_parcels, sorted_cells):
+    kept, moves, total = counts[0, 0], moving(counts), alive(counts)
     for j in range(64):
-        b = order[0, j]
+        b = order[0, jnp.where(j < moves, kept + j, jnp.where(j < total, j - moves, j))]
         sorted_cells[j : j + 1, :] = cells[pl.ds(b, 1), :]
         for k in range(5):
             sorted_parcels[k, j : j + 1, :] = parcels[k, pl.ds(b, 1), :]
 
 
-def alive(counts):
-    return counts[0, 0] + counts[0, 1] + counts[0, 2]
-
-
-def gather_update(counts, box, ahead, own, below, above, parcels, cells, stepped, sources, updated, front, back, fields, table, carried):
-    one, two = sides(own, below, above)
-    stage_two(box, ahead, one, two, stepped, fields)
-    for f in range(5):
-        big, small = two_parts(fields[f])
-        table[pl.ds(32 * f, 32), :] = big
-        table[pl.ds(160 + 32 * f, 32), :] = small
-
-    total = alive(counts)
-
+def gather(table, cells, carried, begin, end):
     def chunk(n, _):
         start = pl.multiple_of(8 * n, 8)
         index = cells[pl.ds(start, 8), :]
@@ -333,37 +349,66 @@
             carried[f, pl.ds(start, 8), :] = jnp.concatenate(values[f], axis=0)
         return 0
 
-    lax.fori_loop(0, (total + 7) // 8, chunk, 0)
-
-    g = tuple(carried[k] for k in range(3))
-    t, y = carried[3], carried[4]
-    v = tuple(parcels[k] for k in range(3))
-    mass, heat = parcels[3], parcels[4]
+    lax.fori_loop(begin, end, chunk, 0)
+
+
+def parcel_update(carried, parcels, rows):
+    g = tuple(carried[k, :rows] for k in range(3))
+    t, y = carried[3, :rows], carried[4, :rows]
+    v = tuple(parcels[k, :rows] for k in range(3))
+    mass, heat = parcels[3, :rows], parcels[4, :rows]
     root = jnp.sqrt(mass)
     inv_root = 1.0 / root
     new_mass = mass * jnp.exp((-TIME_STEP * EVAP_RATE) * t / (root * (1.0 + y * y)))
     slow = jnp.exp((-TIME_STEP / DRAG_RELAX_TIME) * inv_root)
     new_v = tuple(gk + (vk - gk) * slow for gk, vk in zip(g, v, strict=True))
     new_heat = t + (heat - t) * jnp.exp((-TIME_STEP / HEATING_RELAX) * inv_root)
-    live = sublane((64, 128)) < total
-    square = v[0] * v[0] + v[1] * v[1] + v[2] * v[2]
-    new_square = new_v[0] * new_v[0] + new_v[1] * new_v[1] + new_v[2] * new_v[2]
+    return (*v, mass, heat), (*new_v, new_mass, new_heat)
+
+
+def parcel_sources(old, new):
+    mass, new_mass = old[3], new[3]
+    square = old[0] * old[0] + old[1] * old[1] + old[2] * old[2]
+    new_square = new[0] * new[0] + new[1] * new[1] + new[2] * new[2]
     gain = [mass - new_mass]
-    gain += [mass * v[k] - new_mass * new_v[k] for k in range(3)]
-    gain += [0.5 * (mass * square - new_mass * new_square) + LIQUID_HEAT * (mass * heat - new_mass * new_heat)]
-    for k in range(5):
-        sources[k] = jnp.where(live, gain[k], 0.0)
-    for k, value in enumerate((*new_v, new_mass, new_heat)):
-        updated[k] = value
-
-    kept, forward, backward = counts[0, 0], counts[0, 1], counts[0, 2]
-    for out, start, size in ((front, kept, forward), (back, kept + forward, backward)):
+    gain += [mass * old[k] - new_mass * new[k] for k in range(3)]
+    gain += [0.5 * (mass * square - new_mass * new_square) + LIQUID_HEAT * (mass * old[4] - new_mass * new[4])]
+    return gain
+
+
+def gas_and_moving(
+    counts, box, ahead, own, even_pairs, odd_pairs, parcels, cells,
+    stepped, table, carried, even_pay, odd_pay, fields, updated,
+):
+    one, two = sides(own, even_pairs, odd_pairs)
+    stage_two(box, ahead, one, two, stepped, fields)
+    for f in range(5):
+        big, small = two_parts(fields[f])
+        table[pl.ds(32 * f, 32), :] = big
+        table[pl.ds(160 + 32 * f, 32), :] = small
+    gather(table, cells, carried, 0, (moving(counts) + 7) // 8)
+    for k, value in enumerate(parcel_update(carried, parcels, 32)[1]):
+        updated[k, 0:32] = value
+        updated[k, 32:48] = jnp.zeros((16, 128), F32)
+
+    even = is_even("gx")
+    forward, backward = counts[0, 1], counts[0, 2]
+    for out, up in ((even_pay, even), (odd_pay, jnp.logical_not(even))):
+        start = jnp.where(up, 0, forward)
         for k in range(5):
             out[k] = updated[k, pl.ds(start, 16), :]
-        out[5] = jnp.full((16, 128), size.astype(F32))
-
-
-def scatter(counts, stepped, sources, cells, gas_out, total):
+        out[5] = jnp.full((16, 128), jnp.where(up, forward, backward).astype(F32))
+
+
+def kept_and_sources(counts, stepped, table, early, parcels, cells, gas_out, updated, carried, sources, total):
+    carried[:, 0:32] = early[...]
+    chunks = (alive(counts) + 7) // 8
+    gather(table, cells, carried, (moving(counts) + 7) // 8, chunks)
+    old, new = parcel_update(carried, parcels, 64)
+    live = sublane((64, 128)) < alive(counts)
+    for k, value in enumerate(parcel_sources(old, new)):
+        sources[k] = jnp.where(live, value, 0.0)
+        updated[k] = new[k]
     total[...] = jnp.zeros(total.shape, F32)
 
     def chunk(n, _):
@@ -394,7 +439,7 @@
         )
         return 0
 
-    lax.fori_loop(0, (alive(counts) + 7) // 8, chunk, 0)
+    lax.fori_loop(0, chunks, chunk, 0)
     for c in range(6):
         k = c % 5
         both = total[32 * k : 32 * k + 32] + total[160 + 32 * k : 192 + 32 * k]
@@ -403,56 +448,63 @@
             gas_out[c, 4 * half : 4 * half + 4] = stepped[c, 4 * half : 4 * half + 4] + added
 
 
-def place(counts, updated, lower, upper, moved):
-    kept = counts[0, 0]
+def place(counts, updated, even_pairs, odd_pairs, moved):
+    kept, moves = counts[0, 0], moving(counts)
     first, last = ends("gx")
-    from_lower = jnp.where(first, 0.0, lower[5, 0, 0]).astype(jnp.int32)
-    from_upper = jnp.where(last, 0.0, upper[5, 0, 0]).astype(jnp.int32)
-    slot = sublane((64, 128))
+    even = is_even("gx")
+    from_lower = jnp.where(first, 0.0, jnp.where(even, odd_pairs[5, 0, 0], even_pairs[5, 0, 0])).astype(jnp.int32)
+    from_upper = jnp.where(last, 0.0, jnp.where(even, even_pairs[5, 0, 0], odd_pairs[5, 0, 0])).astype(jnp.int32)
+    slot = sublane((32, 128))
     near = sublane((16, 128))
     for k in range(5):
-        moved[k] = jnp.where(slot < kept, updated[k], 0.0)
+        moved[k, 0:32] = jnp.where(slot < kept, updated[k, pl.ds(moves, 32), :], 0.0)
+        moved[k, 32:64] = jnp.zeros((32, 128), F32)
     for k in range(5):
-        moved[k, pl.ds(kept, 16), :] = jnp.where(near < from_lower, lower[k], 0.0)
+        lower = jnp.where(even, odd_pairs[k], even_pairs[k])
+        moved[k, pl.ds(kept, 16), :] = jnp.where(near < from_lower, lower, 0.0)
     for k in range(5):
-        moved[k, pl.ds(kept + from_lower, 16), :] = jnp.where(near < from_upper, upper[k], 0.0)
+        upper = jnp.where(even, even_pairs[k], odd_pairs[k])
+        moved[k, pl.ds(kept + from_lower, 16), :] = jnp.where(near < from_upper, upper, 0.0)
 
 
 def body(gas, parcels, home_cell_index, order, counts):
-    xlo = shifted(gas[:, 6:8], "gx", 1)
-    xhi = shifted(gas[:, 0:2], "gx", -1)
+    even = is_even("gx")
+    edges = [
+        lax.dynamic_slice_in_dim(gas, jnp.where(even, near, far), 2, 1) for near, far in ((6, 0), (0, 6))
+    ]
+    x_halo = swapped(edges, "gx")
     sorted_parcels, cells = call(
-        in_order, [(5, 64, 128), ((64, 128), jnp.int32)], [order], [jnp.transpose(parcels, (1, 0, 2)), home_cell_index]
+        in_order,
+        [(5, 64, 128), ((64, 128), jnp.int32)],
+        [order, counts],
+        [jnp.transpose(parcels, (1, 0, 2)), home_cell_index],
     )
-    rows, low, high = call(pack_y, [(6, 4, 8, 128), (6, 3, 8, 128), (6, 3, 8, 128)], [], [gas, xlo, xhi])
-    ylo = shifted(high, "gy", 1)
-    yhi = shifted(low, "gy", -1)
-    box, pay = call(pack_z, [(6, 12, 16, 128), (6, 16, 128)], [], [gas, rows, ylo, yhi])
-    below = shifted(pay, "gz", 1)
-    above = shifted(pay, "gz", -1)
+    rows, *pays = call(pack_y, [(6, 4, 8, 128), (6, 3, 8, 128), (6, 3, 8, 128)], [], [gas, *x_halo, cells])
+    y_halo = swapped(pays, "gy")
+    box, pay = call(pack_z, [(6, 12, 16, 128), (6, 16, 128)], [], [gas, rows, *y_halo])
+    z_halo = swapped([pay, pay], "gz")
     (ahead,) = call(stage_one, [(6, 12, 16, 128)], [], [box])
-    stepped, sources, updated, front, back = call(
-        gather_update,
-        [(6, 8, 8, 128), (5, 64, 128), (5, 64, 128), (6, 16, 128), (6, 16, 128)],
+    stepped, table, carried, *pays = call(
+        gas_and_moving,
+        [(6, 8, 8, 128), ((320, 256), BF16), (5, 32, 128), (6, 16, 128), (6, 16, 128)],
         [counts],
-        [box, ahead, pay, below, above, sorted_parcels, cells],
+        [box, ahead, pay, *z_halo, sorted_parcels, cells],
+        scratch_shapes=[pltpu.VMEM((5, 32, 256), F32), pltpu.VMEM((5, 48, 128), F32)],
+    )
+    arrived = swapped(pays, "gx")
+    gas_out, updated = call(
+        kept_and_sources,
+        [(6, 8, 8, 128), (5, 64, 128)],
+        [counts],
+        [stepped, table, carried, sorted_parcels, cells],
+        to=[pltpu.HBM, pltpu.VMEM],
         scratch_shapes=[
-            pltpu.VMEM((5, 32, 256), F32),
-            pltpu.VMEM((320, 256), BF16),
             pltpu.VMEM((5, 64, 128), F32),
+            pltpu.VMEM((5, 64, 128), F32),
+            pltpu.VMEM((320, 256), F32),
         ],
     )
-    lower = shifted(front, "gx", 1)
-    upper = shifted(back, "gx", -1)
-    (gas_out,) = call(
-        scatter,
-        [(6, 8, 8, 128)],
-        [counts],
-        [stepped, sources, cells],
-        to=pltpu.HBM,
-        scratch_shapes=[pltpu.VMEM((320, 256), F32)],
-    )
-    (moved,) = call(place, [(5, 64, 128)], [counts], [updated, lower, upper], to=pltpu.HBM)
+    (moved,) = call(place, [(5, 64, 128)], [counts], [updated, *arrived], to=[pltpu.HBM])
     return gas_out, jnp.transpose(moved, (1, 0, 2))
 
 

time: 57.2 us -> 53.2 us (0.930)
  the two profiles are of different devices: /device:TPU:27 before, /device:TPU:30 now
where the time goes in v3:
time: 53.2 us; the launch traced here: 52.8 us
  starting transfers between devices  29.7 us (56%)
  waiting for transfers between devices  11.6 us (22%)
  Pallas kernels  9.82 us (18%)
  local copies, waits for them, and re-layouts  0.93 us (2%)
  between operations  0.8 us (2%)
    ppermute x8, starting transfers between devices, swapped(): out.append(lax.ppermute(block, axis, pairs + [(j, i) for i, j in pairs]))  29.7 us
    ppermute x8, waiting for transfers between devices, swapped(): out.append(lax.ppermute(block, axis, pairs + [(j, i) for i, j in pairs]))  11.6 us
    pallas_call x7, Pallas kernels, call(): pl.pallas_call(kernel, out_shape=[space(*out) for space, out in zip(to, o...  9.82 us
  transfers between devices with their start and end apart: 8, of which 4 were waited for; matrix products, arithmetic and copies ran while one was open for 0% of the time, Pallas kernels for 11%

profile of v3, /device:TPU:30, one launch (start us, length us, event | category | flops | bytes accessed | tf_op | source)
XLA Modules:
  0.0 52.8 jit_solution(18254022968881430123)
XLA Ops:
  0.6 0.0 copy-start.1
  0.7 0.0 copy-start.2
  0.7 0.0 copy-start
  0.7 0.9 %constant_dynamic-slice_fusion = (f32[6,2,8,128]{3,2,1,0:T(8,128)S(1)}, f32[6,2,8,128]{3,2,1,0:T(8,128)S(1)}) fusion(f32[6,8,8,128]{3,2,1,0:T(8,128)} %gas.3, s32[]{:T(128)S(6)} %select_n.18, s32[]{:T(128)S(6)} %select_n.17), kind=kLoop, calls=%fused_computation | loop fusion | bytes 196616 | tf_op jit(solution)/shard_map/dynamic_slice | solution.py:473
  1.6 11.2 %collective-permute-start.1 = (f32[6,2,8,128]{3,2,1,0:T(8,128)S(1)}, f32[6,2,8,128]{3,2,1,0:T(8,128)S(1)}, u32[]{:S(2)}, u32[]{:S(2)}) collective-permute-start(f32[6,2,8,128]{3,2,1,0:T(8,128)S(1)} %get-tuple-element.30), channel_id=1, source_target_pairs={{32,64},{96,128},{160,192},{224,256},{288,320},{352,384},{416,448}... | collective-permute-start | bytes 147464 | tf_op jit(solution)/shard_map/ppermute | solution.py:29
  12.8 1.9 %collective-permute-start = (f32[6,2,8,128]{3,2,1,0:T(8,128)S(1)}, f32[6,2,8,128]{3,2,1,0:T(8,128)S(1)}, u32[]{:S(2)}, u32[]{:S(2)}) collective-permute-start(f32[6,2,8,128]{3,2,1,0:T(8,128)S(1)} %get-tuple-element.31), channel_id=1, source_target_pairs={{0,32},{64,96},{128,160},{192,224},{256,288},{320,352},{384,416},{... | collective-permute-start | bytes 147464 | tf_op jit(solution)/shard_map/ppermute | solution.py:29
  14.7 0.0 copy-done.1
  14.7 0.0 copy-done.2
  14.7 0.9 %shard_map.68 = (f32[5,64,128]{2,1,0:T(8,128)S(1)}, s32[64,128]{1,0:T(8,128)S(1)}) custom-call(s32[1,64]{1,0:T(1,128)} %order.1, s32[1,3]{1,0:T(1,128)} %counts.7, f32[5,64,128]{2,1,0:T(8,128)S(1)} %bitcast.2, s32[64,128]{1,0:T(8,128)S(1)} %copy-done.2), custom_call_target="tpu_custom_call" | custom-call | tf_op jit(solution)/shard_map/pallas_call | solution.py:49
  15.6 0.0 collective-permute-done.1.odd_pairs
  15.7 3.1 %collective-permute-done.even_pairs = f32[6,2,8,128]{3,2,1,0:T(8,128)S(1)} collective-permute-done((f32[6,2,8,128]{3,2,1,0:T(8,128)S(1)}, f32[6,2,8,128]{3,2,1,0:T(8,128)S(1)}, u32[]{:S(2)}, u32[]{:S(2)}) %collective-permute-start) | collective-permute-done | bytes 49184 | tf_op jit(solution)/shard_map/ppermute | solution.py:29
  18.8 0.0 copy-done
  18.8 1.9 %collective-permute-start.2 = (f32[6,3,8,128]{3,2,1,0:T(8,128)S(1)}, f32[6,3,8,128]{3,2,1,0:T(8,128)S(1)}, u32[]{:S(2)}, u32[]{:S(2)}) collective-permute-start(f32[6,3,8,128]{3,2,1,0:T(8,128)S(1)} %get-tuple-element.18), channel_id=1, source_target_pairs={{0,8},{16,24},{8,0},{24,16},{1,9},{17,25},{9,1},{25,17},{2,10},{18... | collective-permute-start | bytes 221192 | tf_op jit(solution)/shard_map/ppermute | solution.py:29
  20.8 3.1 %collective-permute-start.3 = (f32[6,3,8,128]{3,2,1,0:T(8,128)S(1)}, f32[6,3,8,128]{3,2,1,0:T(8,128)S(1)}, u32[]{:S(2)}, u32[]{:S(2)}) collective-permute-start(f32[6,3,8,128]{3,2,1,0:T(8,128)S(1)} %get-tuple-element.19), channel_id=1, source_target_pairs={{8,16},{16,8},{9,17},{17,9},{10,18},{18,10},{11,19},{19,11},{12,20... | collective-permute-start | bytes 221192 | tf_op jit(solution)/shard_map/ppermute | solution.py:29
  23.9 0.0 collective-permute-done.2.even_pairs
  23.9 4.0 %collective-permute-done.3.odd_pairs = f32[6,3,8,128]{3,2,1,0:T(8,128)S(1)} collective-permute-done((f32[6,3,8,128]{3,2,1,0:T(8,128)S(1)}, f32[6,3,8,128]{3,2,1,0:T(8,128)S(1)}, u32[]{:S(2)}, u32[]{:S(2)}) %collective-permute-start.3) | collective-permute-done | bytes 73760 | tf_op jit(solution)/shard_map/ppermute | solution.py:29
  27.9 0.2 shard_map.70
  28.2 4.7 %collective-permute-start.5 = (f32[6,16,128]{2,1,0:T(8,128)S(1)}, f32[6,16,128]{2,1,0:T(8,128)S(1)}, u32[]{:S(2)}, u32[]{:S(2)}) collective-permute-start(f32[6,16,128]{2,1,0:T(8,128)S(1)} %get-tuple-element.21.own), channel_id=1, source_target_pairs={{1,2},{3,4},{5,6},{2,1},{4,3},{6,5},{9,10},{11,12},{13,14},{10,9},... | collective-permute-start | bytes 147464 | tf_op jit(solution)/shard_map/ppermute | solution.py:29
  32.9 1.9 %collective-permute-start.4 = (f32[6,16,128]{2,1,0:T(8,128)S(1)}, f32[6,16,128]{2,1,0:T(8,128)S(1)}, u32[]{:S(2)}, u32[]{:S(2)}) collective-permute-start(f32[6,16,128]{2,1,0:T(8,128)S(1)} %get-tuple-element.21.own), channel_id=1, source_target_pairs={{0,1},{2,3},{4,5},{6,7},{1,0},{3,2},{5,4},{7,6},{8,9},{10,11},{12,... | collective-permute-start | bytes 147464 | tf_op jit(solution)/shard_map/ppermute | solution.py:29
  34.8 0.9 %shard_map.71.ahead = f32[6,12,16,128]{3,2,1,0:T(8,128)S(1)} custom-call(f32[6,12,16,128]{3,2,1,0:T(8,128)S(1)} %get-tuple-element.20.box), custom_call_target="tpu_custom_call" | custom-call | tf_op jit(solution)/shard_map/pallas_call | solution.py:49
  35.7 0.0 collective-permute-done.5.odd_pairs
  35.7 3.1 %collective-permute-done.4.even_pairs = f32[6,16,128]{2,1,0:T(8,128)S(1)} collective-permute-done((f32[6,16,128]{2,1,0:T(8,128)S(1)}, f32[6,16,128]{2,1,0:T(8,128)S(1)}, u32[]{:S(2)}, u32[]{:S(2)}) %collective-permute-start.4) | collective-permute-done | bytes 49184 | tf_op jit(solution)/shard_map/ppermute | solution.py:29
  38.9 2.6 %shard_map.72 = (f32[6,8,8,128]{3,2,1,0:T(8,128)S(1)}, bf16[320,256]{1,0:T(8,128)(2,1)S(1)}, f32[5,32,128]{2,1,0:T(8,128)S(1)}, f32[6,16,128]{2,1,0:T(8,128)S(1)}, f32[6,16,128]{2,1,0:T(8,128)S(1)}) custom-call(s32[1,3]{1,0:T(1,128)} %counts.7, f32[6,12,16,128]{3,2,1,0:T(8,128)S(1)} %get-tuple-element.20.box, f32[6,12,16,128]{3,2,1,0:T(8,128)S(1)} %shard_map.71.ahead, ...), custom_call_target="tpu_custom_call" | custom-call | tf_op jit(solution)/shard_map/pallas_call | solution.py:49
  41.4 1.9 %collective-permute-start.6 = (f32[6,16,128]{2,1,0:T(8,128)S(1)}, f32[6,16,128]{2,1,0:T(8,128)S(1)}, u32[]{:S(2)}, u32[]{:S(2)}) collective-permute-start(f32[6,16,128]{2,1,0:T(8,128)S(1)} %get-tuple-element.28), channel_id=1, source_target_pairs={{0,32},{64,96},{128,160},{192,224},{256,288},{320,352},{384,416},{... | collective-permute-start | bytes 147464 | tf_op jit(solution)/shard_map/ppermute | solution.py:29
  43.4 3.0 %collective-permute-start.7 = (f32[6,16,128]{2,1,0:T(8,128)S(1)}, f32[6,16,128]{2,1,0:T(8,128)S(1)}, u32[]{:S(2)}, u32[]{:S(2)}) collective-permute-start(f32[6,16,128]{2,1,0:T(8,128)S(1)} %get-tuple-element.29), channel_id=1, source_target_pairs={{32,64},{96,128},{160,192},{224,256},{288,320},{352,384},{416,448}... | collective-permute-start | bytes 147464 | tf_op jit(solution)/shard_map/ppermute | solution.py:29
  46.4 3.8 %shard_map.73 = (f32[6,8,8,128]{3,2,1,0:T(8,128)}, f32[5,64,128]{2,1,0:T(8,128)S(1)}) custom-call(s32[1,3]{1,0:T(1,128)} %counts.7, f32[6,8,8,128]{3,2,1,0:T(8,128)S(1)} %get-tuple-element.23.stepped, bf16[320,256]{1,0:T(8,128)(2,1)S(1)} %get-tuple-element.24.table, f32[5,32,128]{2,1,0:T(8,128)S(1)} %get-tuple-element.25.early, ...), custom_call_target="tpu_custom_call" | custom-call | tf_op jit(solution)/shard_map/pallas_call | solution.py:49
  50.2 0.0 collective-permute-done.6.even_pairs
  50.2 1.3 %collective-permute-done.7.odd_pairs = f32[6,16,128]{2,1,0:T(8,128)S(1)} collective-permute-done((f32[6,16,128]{2,1,0:T(8,128)S(1)}, f32[6,16,128]{2,1,0:T(8,128)S(1)}, u32[]{:S(2)}, u32[]{:S(2)}) %collective-permute-start.7) | collective-permute-done | bytes 49184 | tf_op jit(solution)/shard_map/ppermute | solution.py:29
  51.5 1.4 %shard_map.74 = f32[5,64,128]{2,1,0:T(8,128)} custom-call(s32[1,3]{1,0:T(1,128)} %counts.7, f32[5,64,128]{2,1,0:T(8,128)S(1)} %get-tuple-element.27.updated, f32[6,16,128]{2,1,0:T(8,128)S(1)} %collective-permute-done.6.even_pairs, f32[6,16,128]{2,1,0:T(8,128)S(1)} %collective-permute-done.7.odd_pairs), custom_call_target="tpu_custom_call" | custom-call | tf_op jit(solution)/shard_map/pallas_call | solution.py:49
  (1 shorter events, 0.0 us)
Async XLA Ops:
  0.6 14.1 %copy-start.1 = (f32[64,5,128]{2,0,1:T(8,128)S(1)}, f32[64,5,128]{2,0,1:T(8,128)}, u32[]{:S(2)}) copy-start(f32[64,5,128]{2,0,1:T(8,128)} %param.6) | copy-start | bytes 491524
  0.7 14.1 %copy-start.2 = (s32[64,128]{1,0:T(8,128)S(1)}, s32[64,128]{1,0:T(8,128)}, u32[]{:S(2)}) copy-start(s32[64,128]{1,0:T(8,128)} %cells.1) | copy-start | bytes 98308
  0.7 18.1 %copy-start = (f32[6,8,8,128]{3,2,1,0:T(8,128)S(1)}, f32[6,8,8,128]{3,2,1,0:T(8,128)}, u32[]{:S(2)}) copy-start(f32[6,8,8,128]{3,2,1,0:T(8,128)} %gas.3) | copy-start | bytes 589828
  1.6 14.1 %collective-permute-start.1 = (f32[6,2,8,128]{3,2,1,0:T(8,128)S(1)}, f32[6,2,8,128]{3,2,1,0:T(8,128)S(1)}, u32[]{:S(2)}, u32[]{:S(2)}) collective-permute-start(f32[6,2,8,128]{3,2,1,0:T(8,128)S(1)} %get-tuple-element.30), channel_id=1, source_target_pairs={{32,64},{96,128},{160,192},{224,256},{288,320},{352,384},{416,448}... | collective-permute-start | bytes 147464 | tf_op jit(solution)/shard_map/ppermute | solution.py:29
  12.8 6.0 %collective-permute-start = (f32[6,2,8,128]{3,2,1,0:T(8,128)S(1)}, f32[6,2,8,128]{3,2,1,0:T(8,128)S(1)}, u32[]{:S(2)}, u32[]{:S(2)}) collective-permute-start(f32[6,2,8,128]{3,2,1,0:T(8,128)S(1)} %get-tuple-element.31), channel_id=1, source_target_pairs={{0,32},{64,96},{128,160},{192,224},{256,288},{320,352},{384,416},{... | collective-permute-start | bytes 147464 | tf_op jit(solution)/shard_map/ppermute | solution.py:29
  18.8 5.1 %collective-permute-start.2 = (f32[6,3,8,128]{3,2,1,0:T(8,128)S(1)}, f32[6,3,8,128]{3,2,1,0:T(8,128)S(1)}, u32[]{:S(2)}, u32[]{:S(2)}) collective-permute-start(f32[6,3,8,128]{3,2,1,0:T(8,128)S(1)} %get-tuple-element.18), channel_id=1, source_target_pairs={{0,8},{16,24},{8,0},{24,16},{1,9},{17,25},{9,1},{25,17},{2,10},{18... | collective-permute-start | bytes 221192 | tf_op jit(solution)/shard_map/ppermute | solution.py:29
  20.8 7.2 %collective-permute-start.3 = (f32[6,3,8,128]{3,2,1,0:T(8,128)S(1)}, f32[6,3,8,128]{3,2,1,0:T(8,128)S(1)}, u32[]{:S(2)}, u32[]{:S(2)}) collective-permute-start(f32[6,3,8,128]{3,2,1,0:T(8,128)S(1)} %get-tuple-element.19), channel_id=1, source_target_pairs={{8,16},{16,8},{9,17},{17,9},{10,18},{18,10},{11,19},{19,11},{12,20... | collective-permute-start | bytes 221192 | tf_op jit(solution)/shard_map/ppermute | solution.py:29
  28.2 7.5 %collective-permute-start.5 = (f32[6,16,128]{2,1,0:T(8,128)S(1)}, f32[6,16,128]{2,1,0:T(8,128)S(1)}, u32[]{:S(2)}, u32[]{:S(2)}) collective-permute-start(f32[6,16,128]{2,1,0:T(8,128)S(1)} %get-tuple-element.21.own), channel_id=1, source_target_pairs={{1,2},{3,4},{5,6},{2,1},{4,3},{6,5},{9,10},{11,12},{13,14},{10,9},... | collective-permute-start | bytes 147464 | tf_op jit(solution)/shard_map/ppermute | solution.py:29
  32.9 6.0 %collective-permute-start.4 = (f32[6,16,128]{2,1,0:T(8,128)S(1)}, f32[6,16,128]{2,1,0:T(8,128)S(1)}, u32[]{:S(2)}, u32[]{:S(2)}) collective-permute-start(f32[6,16,128]{2,1,0:T(8,128)S(1)} %get-tuple-element.21.own), channel_id=1, source_target_pairs={{0,1},{2,3},{4,5},{6,7},{1,0},{3,2},{5,4},{7,6},{8,9},{10,11},{12,... | collective-permute-start | bytes 147464 | tf_op jit(solution)/shard_map/ppermute | solution.py:29
  41.4 8.8 %collective-permute-start.6 = (f32[6,16,128]{2,1,0:T(8,128)S(1)}, f32[6,16,128]{2,1,0:T(8,128)S(1)}, u32[]{:S(2)}, u32[]{:S(2)}) collective-permute-start(f32[6,16,128]{2,1,0:T(8,128)S(1)} %get-tuple-element.28), channel_id=1, source_target_pairs={{0,32},{64,96},{128,160},{192,224},{256,288},{320,352},{384,416},{... | collective-permute-start | bytes 147464 | tf_op jit(solution)/shard_map/ppermute | solution.py:29
  43.4 8.1 %collective-permute-start.7 = (f32[6,16,128]{2,1,0:T(8,128)S(1)}, f32[6,16,128]{2,1,0:T(8,128)S(1)}, u32[]{:S(2)}, u32[]{:S(2)}) collective-permute-start(f32[6,16,128]{2,1,0:T(8,128)S(1)} %get-tuple-element.29), channel_id=1, source_target_pairs={{32,64},{96,128},{160,192},{224,256},{288,320},{352,384},{416,448}... | collective-permute-start | bytes 147464 | tf_op jit(solution)/shard_map/ppermute | solution.py:29

commit v4 on v3

--- a/solution.py
+++ b/solution.py
@@ -314,16 +314,16 @@
     return jnp.where(sublane((count, index.shape[-1])) == index, 1.0, 0.0).astype(BF16)
 
 
-def moving(counts):
-    return counts[0, 1] + counts[0, 2]
-
-
-def alive(counts):
-    return counts[0, 0] + moving(counts)
-
-
-def in_order(order, counts, parcels, cells, sorted_parcels, sorted_cells):
-    kept, moves, total = counts[0, 0], moving(counts), alive(counts)
+def numbers(info):
+    return info[0, 0], info[1, 0], info[2, 0]
+
+
+def in_order(order, counts, parcels, cells, sorted_parcels, sorted_cells, info):
+    kept, forward, backward = counts[0, 0], counts[0, 1], counts[0, 2]
+    moves, total = forward + backward, kept + forward + backward
+    for k, number in enumerate((kept, forward, backward)):
+        info[k : k + 1, :] = jnp.full((1, 128), number)
+    info[3:8, :] = jnp.zeros((5, 128), jnp.int32)
     for j in range(64):
         b = order[0, jnp.where(j < moves, kept + j, jnp.where(j < total, j - moves, j))]
         sorted_cells[j : j + 1, :] = cells[pl.ds(b, 1), :]
@@ -377,22 +377,22 @@
 
 
 def gas_and_moving(
-    counts, box, ahead, own, even_pairs, odd_pairs, parcels, cells,
+    info, box, ahead, own, even_pairs, odd_pairs, parcels, cells,
     stepped, table, carried, even_pay, odd_pay, fields, updated,
 ):
+    _, forward, backward = numbers(info)
     one, two = sides(own, even_pairs, odd_pairs)
     stage_two(box, ahead, one, two, stepped, fields)
     for f in range(5):
         big, small = two_parts(fields[f])
         table[pl.ds(32 * f, 32), :] = big
         table[pl.ds(160 + 32 * f, 32), :] = small
-    gather(table, cells, carried, 0, (moving(counts) + 7) // 8)
+    gather(table, cells, carried, 0, (forward + backward + 7) // 8)
     for k, value in enumerate(parcel_update(carried, parcels, 32)[1]):
         updated[k, 0:32] = value
         updated[k, 32:48] = jnp.zeros((16, 128), F32)
 
     even = is_even("gx")
-    forward, backward = counts[0, 1], counts[0, 2]
     for out, up in ((even_pay, even), (odd_pay, jnp.logical_not(even))):
         start = jnp.where(up, 0, forward)
         for k in range(5):
@@ -400,12 +400,14 @@
         out[5] = jnp.full((16, 128), jnp.where(up, forward, backward).astype(F32))
 
 
-def kept_and_sources(counts, stepped, table, early, parcels, cells, gas_out, updated, carried, sources, total):
+def kept_and_sources(info, stepped, table, early, parcels, cells, gas_out, updated, carried, sources, total):
+    kept, forward, backward = numbers(info)
+    moves = forward + backward
+    chunks = (kept + moves + 7) // 8
     carried[:, 0:32] = early[...]
-    chunks = (alive(counts) + 7) // 8
-    gather(table, cells, carried, (moving(counts) + 7) // 8, chunks)
+    gather(table, cells, carried, (moves + 7) // 8, chunks)
     old, new = parcel_update(carried, parcels, 64)
-    live = sublane((64, 128)) < alive(counts)
+    live = sublane((64, 128)) < kept + moves
     for k, value in enumerate(parcel_sources(old, new)):
         sources[k] = jnp.where(live, value, 0.0)
         updated[k] = new[k]
@@ -448,8 +450,10 @@
             gas_out[c, 4 * half : 4 * half + 4] = stepped[c, 4 * half : 4 * half + 4] + added
 
 
-def place(counts, updated, even_pairs, odd_pairs, moved):
-    kept, moves = counts[0, 0], moving(counts)
+def place(info, updated, even_pairs, odd_pairs, gas, moved, gas_out):
+    kept, forward, backward = numbers(info)
+    moves = forward + backward
+    gas_out[...] = gas[...]
     first, last = ends("gx")
     even = is_even("gx")
     from_lower = jnp.where(first, 0.0, jnp.where(even, odd_pairs[5, 0, 0], even_pairs[5, 0, 0])).astype(jnp.int32)
@@ -473,9 +477,9 @@
         lax.dynamic_slice_in_dim(gas, jnp.where(even, near, far), 2, 1) for near, far in ((6, 0), (0, 6))
     ]
     x_halo = swapped(edges, "gx")
-    sorted_parcels, cells = call(
+    sorted_parcels, cells, info = call(
         in_order,
-        [(5, 64, 128), ((64, 128), jnp.int32)],
+        [(5, 64, 128), ((64, 128), jnp.int32), ((8, 128), jnp.int32)],
         [order, counts],
         [jnp.transpose(parcels, (1, 0, 2)), home_cell_index],
     )
@@ -487,24 +491,25 @@
     stepped, table, carried, *pays = call(
         gas_and_moving,
         [(6, 8, 8, 128), ((320, 256), BF16), (5, 32, 128), (6, 16, 128), (6, 16, 128)],
-        [counts],
-        [box, ahead, pay, *z_halo, sorted_parcels, cells],
+        [],
+        [info, box, ahead, pay, *z_halo, sorted_parcels, cells],
         scratch_shapes=[pltpu.VMEM((5, 32, 256), F32), pltpu.VMEM((5, 48, 128), F32)],
     )
     arrived = swapped(pays, "gx")
-    gas_out, updated = call(
+    gas_done, updated = call(
         kept_and_sources,
         [(6, 8, 8, 128), (5, 64, 128)],
-        [counts],
-        [stepped, table, carried, sorted_parcels, cells],
-        to=[pltpu.HBM, pltpu.VMEM],
+        [],
+        [info, stepped, table, carried, sorted_parcels, cells],
         scratch_shapes=[
             pltpu.VMEM((5, 64, 128), F32),
             pltpu.VMEM((5, 64, 128), F32),
             pltpu.VMEM((320, 256), F32),
         ],
     )
-    (moved,) = call(place, [(5, 64, 128)], [counts], [updated, *arrived], to=[pltpu.HBM])
+    moved, gas_out = call(
+        place, [(5, 64, 128), (6, 8, 8, 128)], [], [info, updated, *arrived, gas_done], to=[pltpu.HBM] * 2
+    )
     return gas_out, jnp.transpose(moved, (1, 0, 2))
 
 

time: 53.2 us -> 51.9 us (0.976)
  Pallas kernels: 9.82 us -> 7.28 us
  waiting for transfers between devices: 11.6 us -> 12.8 us
    pallas_call x7, Pallas kernels: 9.82 us -> 7.28 us  [call(): pl.pallas_call(kernel, out_shape=[space(*out) for space, out in zip(to, o...]
    ppermute x8, waiting for transfers between devices: 11.6 us -> 12.8 us  [swapped(): out.append(lax.ppermute(block, axis, pairs + [(j, i) for i, j in pairs]))]
  transfers between devices with their start and end apart: 8 -> 8, of which waited for: 4 -> 4; matrix products, arithmetic and copies ran while one was open for 0% -> 0% of each run, Pallas kernels for 11% -> 8%
where the time goes in v4:
time: 51.9 us; the launch traced here: 51.6 us
  starting transfers between devices  29.7 us (57%)
  waiting for transfers between devices  12.8 us (25%)
  Pallas kernels  7.28 us (14%)
  local copies, waits for them, and re-layouts  0.93 us (2%)
  between operations  0.81 us (2%)
    ppermute x8, starting transfers between devices, swapped(): out.append(lax.ppermute(block, axis, pairs + [(j, i) for i, j in pairs]))  29.7 us
    ppermute x8, waiting for transfers between devices, swapped(): out.append(lax.ppermute(block, axis, pairs + [(j, i) for i, j in pairs]))  12.8 us
    pallas_call x7, Pallas kernels, call(): pl.pallas_call(kernel, out_shape=[space(*out) for space, out in zip(to, o...  7.28 us
  transfers between devices with their start and end apart: 8, of which 4 were waited for; matrix products, arithmetic and copies ran while one was open for 0% of the time, Pallas kernels for 8%

profile of v4, /device:TPU:30, one launch (start us, length us, event | category | flops | bytes accessed | tf_op | source)
XLA Modules:
  0.0 51.6 jit_solution(13915649152891234743)
XLA Ops:
  0.6 0.0 copy-start.1
  0.7 0.0 copy-start.2
  0.7 0.0 copy-start
  0.7 0.9 %constant_dynamic-slice_fusion = (f32[6,2,8,128]{3,2,1,0:T(8,128)S(1)}, f32[6,2,8,128]{3,2,1,0:T(8,128)S(1)}) fusion(f32[6,8,8,128]{3,2,1,0:T(8,128)} %gas.3, s32[]{:T(128)S(6)} %select_n.18, s32[]{:T(128)S(6)} %select_n.17), kind=kLoop, calls=%fused_computation | loop fusion | bytes 196616 | tf_op jit(solution)/shard_map/dynamic_slice | solution.py:477
  1.6 11.2 %collective-permute-start.1 = (f32[6,2,8,128]{3,2,1,0:T(8,128)S(1)}, f32[6,2,8,128]{3,2,1,0:T(8,128)S(1)}, u32[]{:S(2)}, u32[]{:S(2)}) collective-permute-start(f32[6,2,8,128]{3,2,1,0:T(8,128)S(1)} %get-tuple-element.36), channel_id=1, source_target_pairs={{32,64},{96,128},{160,192},{224,256},{288,320},{352,384},{416,448}... | collective-permute-start | bytes 147464 | tf_op jit(solution)/shard_map/ppermute | solution.py:29
  12.8 1.9 %collective-permute-start = (f32[6,2,8,128]{3,2,1,0:T(8,128)S(1)}, f32[6,2,8,128]{3,2,1,0:T(8,128)S(1)}, u32[]{:S(2)}, u32[]{:S(2)}) collective-permute-start(f32[6,2,8,128]{3,2,1,0:T(8,128)S(1)} %get-tuple-element.37), channel_id=1, source_target_pairs={{0,32},{64,96},{128,160},{192,224},{256,288},{320,352},{384,416},{... | collective-permute-start | bytes 147464 | tf_op jit(solution)/shard_map/ppermute | solution.py:29
  14.7 0.0 copy-done.1
  14.7 0.0 copy-done.2
  14.7 0.9 %shard_map.68 = (f32[5,64,128]{2,1,0:T(8,128)S(1)}, s32[64,128]{1,0:T(8,128)S(1)}, s32[8,128]{1,0:T(8,128)S(1)}) custom-call(s32[1,64]{1,0:T(1,128)} %order.1, s32[1,3]{1,0:T(1,128)} %counts.1, f32[5,64,128]{2,1,0:T(8,128)S(1)} %bitcast.2, s32[64,128]{1,0:T(8,128)S(1)} %copy-done.2), custom_call_target="tpu_custom_call" | custom-call | tf_op jit(solution)/shard_map/pallas_call | solution.py:49
  15.6 0.0 collective-permute-done.1.odd_pairs
  15.7 3.1 %collective-permute-done.even_pairs = f32[6,2,8,128]{3,2,1,0:T(8,128)S(1)} collective-permute-done((f32[6,2,8,128]{3,2,1,0:T(8,128)S(1)}, f32[6,2,8,128]{3,2,1,0:T(8,128)S(1)}, u32[]{:S(2)}, u32[]{:S(2)}) %collective-permute-start) | collective-permute-done | bytes 49184 | tf_op jit(solution)/shard_map/ppermute | solution.py:29
  18.8 0.0 copy-done
  18.8 1.9 %collective-permute-start.2 = (f32[6,3,8,128]{3,2,1,0:T(8,128)S(1)}, f32[6,3,8,128]{3,2,1,0:T(8,128)S(1)}, u32[]{:S(2)}, u32[]{:S(2)}) collective-permute-start(f32[6,3,8,128]{3,2,1,0:T(8,128)S(1)} %get-tuple-element.22), channel_id=1, source_target_pairs={{0,8},{16,24},{8,0},{24,16},{1,9},{17,25},{9,1},{25,17},{2,10},{18... | collective-permute-start | bytes 221192 | tf_op jit(solution)/shard_map/ppermute | solution.py:29
  20.8 3.1 %collective-permute-start.3 = (f32[6,3,8,128]{3,2,1,0:T(8,128)S(1)}, f32[6,3,8,128]{3,2,1,0:T(8,128)S(1)}, u32[]{:S(2)}, u32[]{:S(2)}) collective-permute-start(f32[6,3,8,128]{3,2,1,0:T(8,128)S(1)} %get-tuple-element.23), channel_id=1, source_target_pairs={{8,16},{16,8},{9,17},{17,9},{10,18},{18,10},{11,19},{19,11},{12,20... | collective-permute-start | bytes 221192 | tf_op jit(solution)/shard_map/ppermute | solution.py:29
  23.9 0.0 collective-permute-done.2.even_pairs
  23.9 4.0 %collective-permute-done.3.odd_pairs = f32[6,3,8,128]{3,2,1,0:T(8,128)S(1)} collective-permute-done((f32[6,3,8,128]{3,2,1,0:T(8,128)S(1)}, f32[6,3,8,128]{3,2,1,0:T(8,128)S(1)}, u32[]{:S(2)}, u32[]{:S(2)}) %collective-permute-start.3) | collective-permute-done | bytes 73760 | tf_op jit(solution)/shard_map/ppermute | solution.py:29
  27.9 0.2 shard_map.70
  28.2 4.7 %collective-permute-start.5 = (f32[6,16,128]{2,1,0:T(8,128)S(1)}, f32[6,16,128]{2,1,0:T(8,128)S(1)}, u32[]{:S(2)}, u32[]{:S(2)}) collective-permute-start(f32[6,16,128]{2,1,0:T(8,128)S(1)} %get-tuple-element.25.own), channel_id=1, source_target_pairs={{1,2},{3,4},{5,6},{2,1},{4,3},{6,5},{9,10},{11,12},{13,14},{10,9},... | collective-permute-start | bytes 147464 | tf_op jit(solution)/shard_map/ppermute | solution.py:29
  32.9 1.9 %collective-permute-start.4 = (f32[6,16,128]{2,1,0:T(8,128)S(1)}, f32[6,16,128]{2,1,0:T(8,128)S(1)}, u32[]{:S(2)}, u32[]{:S(2)}) collective-permute-start(f32[6,16,128]{2,1,0:T(8,128)S(1)} %get-tuple-element.25.own), channel_id=1, source_target_pairs={{0,1},{2,3},{4,5},{6,7},{1,0},{3,2},{5,4},{7,6},{8,9},{10,11},{12,... | collective-permute-start | bytes 147464 | tf_op jit(solution)/shard_map/ppermute | solution.py:29
  34.8 0.9 %shard_map.71.ahead = f32[6,12,16,128]{3,2,1,0:T(8,128)S(1)} custom-call(f32[6,12,16,128]{3,2,1,0:T(8,128)S(1)} %get-tuple-element.24.box), custom_call_target="tpu_custom_call" | custom-call | tf_op jit(solution)/shard_map/pallas_call | solution.py:49
  35.7 0.0 collective-permute-done.5.odd_pairs
  35.7 3.1 %collective-permute-done.4.even_pairs = f32[6,16,128]{2,1,0:T(8,128)S(1)} collective-permute-done((f32[6,16,128]{2,1,0:T(8,128)S(1)}, f32[6,16,128]{2,1,0:T(8,128)S(1)}, u32[]{:S(2)}, u32[]{:S(2)}) %collective-permute-start.4) | collective-permute-done | bytes 49184 | tf_op jit(solution)/shard_map/ppermute | solution.py:29
  38.9 1.9 %shard_map.72 = (f32[6,8,8,128]{3,2,1,0:T(8,128)S(1)}, bf16[320,256]{1,0:T(8,128)(2,1)S(1)}, f32[5,32,128]{2,1,0:T(8,128)S(1)}, f32[6,16,128]{2,1,0:T(8,128)S(1)}, f32[6,16,128]{2,1,0:T(8,128)S(1)}) custom-call(s32[8,128]{1,0:T(8,128)S(1)} %get-tuple-element.19.info, f32[6,12,16,128]{3,2,1,0:T(8,128)S(1)} %get-tuple-element.24.box, ...), custom_call_target="tpu_custom_call" | custom-call | tf_op jit(solution)/shard_map/pallas_call | solution.py:49
  40.8 1.9 %collective-permute-start.6 = (f32[6,16,128]{2,1,0:T(8,128)S(1)}, f32[6,16,128]{2,1,0:T(8,128)S(1)}, u32[]{:S(2)}, u32[]{:S(2)}) collective-permute-start(f32[6,16,128]{2,1,0:T(8,128)S(1)} %get-tuple-element.31), channel_id=1, source_target_pairs={{0,32},{64,96},{128,160},{192,224},{256,288},{320,352},{384,416},{... | collective-permute-start | bytes 147464 | tf_op jit(solution)/shard_map/ppermute | solution.py:29
  42.7 3.0 %collective-permute-start.7 = (f32[6,16,128]{2,1,0:T(8,128)S(1)}, f32[6,16,128]{2,1,0:T(8,128)S(1)}, u32[]{:S(2)}, u32[]{:S(2)}) collective-permute-start(f32[6,16,128]{2,1,0:T(8,128)S(1)} %get-tuple-element.32), channel_id=1, source_target_pairs={{32,64},{96,128},{160,192},{224,256},{288,320},{352,384},{416,448}... | collective-permute-start | bytes 147464 | tf_op jit(solution)/shard_map/ppermute | solution.py:29
  45.7 2.5 %shard_map.73 = (f32[6,8,8,128]{3,2,1,0:T(8,128)S(1)}, f32[5,64,128]{2,1,0:T(8,128)S(1)}) custom-call(s32[8,128]{1,0:T(8,128)S(1)} %get-tuple-element.19.info, f32[6,8,8,128]{3,2,1,0:T(8,128)S(1)} %get-tuple-element.27.stepped, bf16[320,256]{1,0:T(8,128)(2,1)S(1)} %get-tuple-element.28.table, f32[5,32,128]{2,1,0:T(8,128)S(1)} %get-tuple-element.29.early, ...), custom_call_target="tpu_custom_call" | custom-call | tf_op jit(solution)/shard_map/pallas_call | solution.py:49
  48.2 0.0 collective-permute-done.6.even_pairs
  48.3 2.6 %collective-permute-done.7.odd_pairs = f32[6,16,128]{2,1,0:T(8,128)S(1)} collective-permute-done((f32[6,16,128]{2,1,0:T(8,128)S(1)}, f32[6,16,128]{2,1,0:T(8,128)S(1)}, u32[]{:S(2)}, u32[]{:S(2)}) %collective-permute-start.7) | collective-permute-done | bytes 49184 | tf_op jit(solution)/shard_map/ppermute | solution.py:29
  50.8 0.8 %shard_map.74 = (f32[5,64,128]{2,1,0:T(8,128)}, f32[6,8,8,128]{3,2,1,0:T(8,128)}) custom-call(s32[8,128]{1,0:T(8,128)S(1)} %get-tuple-element.19.info, f32[5,64,128]{2,1,0:T(8,128)S(1)} %get-tuple-element.30.updated, f32[6,16,128]{2,1,0:T(8,128)S(1)} %collective-permute-done.6.even_pairs, f32[6,16,128]{2,1,0:T(8,128)S(1)} %collective-permute-done.7.odd_pairs, ...), custom_call_target="tpu_custom_call" | custom-call | tf_op jit(solution)/shard_map/pallas_call | solution.py:49
  (1 shorter events, 0.0 us)
Async XLA Ops:
  0.6 14.1 %copy-start.1 = (f32[64,5,128]{2,0,1:T(8,128)S(1)}, f32[64,5,128]{2,0,1:T(8,128)}, u32[]{:S(2)}) copy-start(f32[64,5,128]{2,0,1:T(8,128)} %param.6) | copy-start | bytes 491524
  0.7 14.1 %copy-start.2 = (s32[64,128]{1,0:T(8,128)S(1)}, s32[64,128]{1,0:T(8,128)}, u32[]{:S(2)}) copy-start(s32[64,128]{1,0:T(8,128)} %cells.1) | copy-start | bytes 98308
  0.7 18.1 %copy-start = (f32[6,8,8,128]{3,2,1,0:T(8,128)S(1)}, f32[6,8,8,128]{3,2,1,0:T(8,128)}, u32[]{:S(2)}) copy-start(f32[6,8,8,128]{3,2,1,0:T(8,128)} %gas.3) | copy-start | bytes 589828
  1.6 14.1 %collective-permute-start.1 = (f32[6,2,8,128]{3,2,1,0:T(8,128)S(1)}, f32[6,2,8,128]{3,2,1,0:T(8,128)S(1)}, u32[]{:S(2)}, u32[]{:S(2)}) collective-permute-start(f32[6,2,8,128]{3,2,1,0:T(8,128)S(1)} %get-tuple-element.36), channel_id=1, source_target_pairs={{32,64},{96,128},{160,192},{224,256},{288,320},{352,384},{416,448}... | collective-permute-start | bytes 147464 | tf_op jit(solution)/shard_map/ppermute | solution.py:29
  12.8 6.0 %collective-permute-start = (f32[6,2,8,128]{3,2,1,0:T(8,128)S(1)}, f32[6,2,8,128]{3,2,1,0:T(8,128)S(1)}, u32[]{:S(2)}, u32[]{:S(2)}) collective-permute-start(f32[6,2,8,128]{3,2,1,0:T(8,128)S(1)} %get-tuple-element.37), channel_id=1, source_target_pairs={{0,32},{64,96},{128,160},{192,224},{256,288},{320,352},{384,416},{... | collective-permute-start | bytes 147464 | tf_op jit(solution)/shard_map/ppermute | solution.py:29
  18.8 5.1 %collective-permute-start.2 = (f32[6,3,8,128]{3,2,1,0:T(8,128)S(1)}, f32[6,3,8,128]{3,2,1,0:T(8,128)S(1)}, u32[]{:S(2)}, u32[]{:S(2)}) collective-permute-start(f32[6,3,8,128]{3,2,1,0:T(8,128)S(1)} %get-tuple-element.22), channel_id=1, source_target_pairs={{0,8},{16,24},{8,0},{24,16},{1,9},{17,25},{9,1},{25,17},{2,10},{18... | collective-permute-start | bytes 221192 | tf_op jit(solution)/shard_map/ppermute | solution.py:29
  20.8 7.2 %collective-permute-start.3 = (f32[6,3,8,128]{3,2,1,0:T(8,128)S(1)}, f32[6,3,8,128]{3,2,1,0:T(8,128)S(1)}, u32[]{:S(2)}, u32[]{:S(2)}) collective-permute-start(f32[6,3,8,128]{3,2,1,0:T(8,128)S(1)} %get-tuple-element.23), channel_id=1, source_target_pairs={{8,16},{16,8},{9,17},{17,9},{10,18},{18,10},{11,19},{19,11},{12,20... | collective-permute-start | bytes 221192 | tf_op jit(solution)/shard_map/ppermute | solution.py:29
  28.2 7.6 %collective-permute-start.5 = (f32[6,16,128]{2,1,0:T(8,128)S(1)}, f32[6,16,128]{2,1,0:T(8,128)S(1)}, u32[]{:S(2)}, u32[]{:S(2)}) collective-permute-start(f32[6,16,128]{2,1,0:T(8,128)S(1)} %get-tuple-element.25.own), channel_id=1, source_target_pairs={{1,2},{3,4},{5,6},{2,1},{4,3},{6,5},{9,10},{11,12},{13,14},{10,9},... | collective-permute-start | bytes 147464 | tf_op jit(solution)/shard_map/ppermute | solution.py:29
  32.9 6.0 %collective-permute-start.4 = (f32[6,16,128]{2,1,0:T(8,128)S(1)}, f32[6,16,128]{2,1,0:T(8,128)S(1)}, u32[]{:S(2)}, u32[]{:S(2)}) collective-permute-start(f32[6,16,128]{2,1,0:T(8,128)S(1)} %get-tuple-element.25.own), channel_id=1, source_target_pairs={{0,1},{2,3},{4,5},{6,7},{1,0},{3,2},{5,4},{7,6},{8,9},{10,11},{12,... | collective-permute-start | bytes 147464 | tf_op jit(solution)/shard_map/ppermute | solution.py:29
  40.8 7.5 %collective-permute-start.6 = (f32[6,16,128]{2,1,0:T(8,128)S(1)}, f32[6,16,128]{2,1,0:T(8,128)S(1)}, u32[]{:S(2)}, u32[]{:S(2)}) collective-permute-start(f32[6,16,128]{2,1,0:T(8,128)S(1)} %get-tuple-element.31), channel_id=1, source_target_pairs={{0,32},{64,96},{128,160},{192,224},{256,288},{320,352},{384,416},{... | collective-permute-start | bytes 147464 | tf_op jit(solution)/shard_map/ppermute | solution.py:29
  42.7 8.1 %collective-permute-start.7 = (f32[6,16,128]{2,1,0:T(8,128)S(1)}, f32[6,16,128]{2,1,0:T(8,128)S(1)}, u32[]{:S(2)}, u32[]{:S(2)}) collective-permute-start(f32[6,16,128]{2,1,0:T(8,128)S(1)} %get-tuple-element.32), channel_id=1, source_target_pairs={{32,64},{96,128},{160,192},{224,256},{288,320},{352,384},{416,448}... | collective-permute-start | bytes 147464 | tf_op jit(solution)/shard_map/ppermute | solution.py:29
